TPU v7x, 256 devices: a whole 4x4x8 slice. The times are simulated.
256 devices in a mesh: theta: 128 (over y_hi, x, z, core), gz: 2 (over y_lo).
Axes of the slice: x: 4, y: 4 (y_hi: 2, y_lo: 2; y = y_hi * 2 + y_lo), z: 8, core: 2. Of those that a mesh axis runs over, the one named last changes fastest.
Arguments:
- field: float32 [16, 8192, 1024], P('gz', 'theta'), parts along dimension 0, may hold values from -6 to 6
- courant: float32 [1024], replicated, may hold values from 0.2 to 0.8
Outputs:
- advanced: float32 [16, 8192, 1024], P('gz', 'theta'), parts along dimension 0
There are 2 independent parts, one for each index of `gz`. A program takes and returns all parts, laid end to end along the dimension named above; an argument that names none is the same for every part. Nothing has to cross between parts.
All inputs are finite; a program needn't handle non-finite values.
Results may differ from a plain program's by a relative error of at most 0.00007.
Values sent between devices are 32-bit elements; how exact they have to be, the bound alone decides.
No kernel may reach another device: no remote copies, remote signals or barrier semaphores. Data moves between devices by JAX's collectives and lax.ppermute only.
A program may use at most 128 MiB of HBM per device.

v0:
```python
import functools
import math

import jax
import jax.numpy as jnp
import ml_dtypes
import numpy as np
from jax import lax
from jax.experimental import pallas as pl
from jax.experimental.pallas import tpu as pltpu
from jax.sharding import PartitionSpec as P

stencil_weights = (4.0 / 5.0, -1.0 / 5.0, 4.0 / 105.0, -1.0 / 280.0)
radial_step = 0.2
rank = 24
lines = 8
halo = 12
f32 = jnp.float32
bf16 = jnp.bfloat16


def split_table(a):
    hi = a.astype(ml_dtypes.bfloat16)
    lo = (a - hi.astype(np.float64)).astype(ml_dtypes.bfloat16)
    return hi, lo


def cross_factors(block, terms):
    rest = block.copy()
    left, right = [], []
    for _ in range(terms):
        at = np.unravel_index(np.argmax(np.abs(rest)), rest.shape)
        column = rest[:, at[1]] / rest[at]
        row = rest[at[0], :].copy()
        left.append(column)
        right.append(row)
        rest = rest - column[:, None] * row[None, :]
    return np.stack(left, axis=1), np.stack(right, axis=0)


@functools.lru_cache(maxsize=None)
def tables(count):
    intervals = 2 * count - 1
    row = np.arange(count)[:, None]
    col = np.arange(2 * count)[None, :]
    sines = np.array([math.sin(math.pi * k / (2 * intervals)) for k in range(3 * count)])
    same = row == col
    spacing = -2.0 * sines[row + col] * np.sign(row - col) * sines[np.abs(row - col)]
    row_factor = np.where(row == 0, 2.0, 1.0)
    col_factor = np.where((col == 0) | (col == intervals), 2.0, 1.0)
    parity = np.where((row + col) % 2 == 0, 1.0, -1.0)
    off = np.where(same, 0.0, row_factor / col_factor * parity / np.where(same, 1.0, spacing))
    matrix = off - np.where(same, off.sum(axis=1, keepdims=True), 0.0)
    near = matrix[:, :count].T
    far = matrix[:, count:][:, ::-1].T
    scale = -(radial_step / intervals) * sines[2 * np.arange(count)] ** 2
    left, right = cross_factors(far, rank)
    near_hi, near_lo = split_table(near * scale[None, :])
    left_hi, left_lo = split_table(left)
    right_hi, right_lo = split_table(right * scale[None, :])
    left_both = np.zeros((count, 128), ml_dtypes.bfloat16)
    left_both[:, :rank] = left_hi
    left_both[:, rank : 2 * rank] = left_lo
    right_all = np.concatenate([right_hi, right_hi, right_lo, right_lo], axis=0)
    return near_hi, near_lo, left_both, right_all


def halves(x):
    hi = x.astype(bf16)
    lo = (x - hi.astype(f32)).astype(bf16)
    return hi, lo


def dot(a, b):
    return jnp.dot(a, b, preferred_element_type=f32)


def near_product(hi, lo, near_hi, near_lo):
    return dot(hi, near_hi) + dot(lo, near_hi) + dot(hi, near_lo)


def projected(hi, lo, left_both):
    both = (dot(hi, left_both) + dot(lo, left_both)).T
    return both[:rank] + both[rank : 2 * rank]


def edges_kernel(par, field, to_pair, to_other):
    first = [jnp.swapaxes(field[:, 0:16, :], 0, 1)[:halo].reshape(halo * lines, -1)]
    last = [jnp.swapaxes(field[:, 48:64, :], 0, 1)[16 - halo :].reshape(halo * lines, -1)]

    @pl.when(par[0] == 0)
    def _():
        to_pair[...] = last[0]
        to_other[...] = first[0]

    @pl.when(par[0] != 0)
    def _():
        to_pair[...] = first[0]
        to_other[...] = last[0]


def own_kernel(field, near_hi, near_lo, left_both, state, product, proj):
    for at in range(0, 64, 16):
        rows = jnp.swapaxes(field[:, at : at + 16, :], 0, 1).reshape(16 * lines, -1)
        span = slice(at * lines, (at + 16) * lines)
        state[span, :] = rows
        hi, lo = halves(rows)
        product[span, :] = near_product(hi, lo, near_hi[...], near_lo[...])
        proj[:, span] = projected(hi, lo, left_both[...])


def join_kernel(par, own, proj_own, from_pair, from_other, left_both, state, proj):
    wide = halo * lines
    total = own.shape[0]
    state[wide : wide + total, :] = own[...]

    @pl.when(par[0] == 0)
    def _():
        state[:wide, :] = from_other[...]
        state[wide + total :, :] = from_pair[...]

    @pl.when(par[0] != 0)
    def _():
        state[:wide, :] = from_pair[...]
        state[wide + total :, :] = from_other[...]

    rows = jnp.concatenate([state[32:wide, :], state[wide + total : wide + total + 64, :]], axis=0)
    hi, lo = halves(rows)
    proj[:, :total] = proj_own[...]
    proj[:, total:] = projected(hi, lo, left_both[...])


def azimuth(state, courant, start, count):
    window = state[start : start + count + 64, :]
    total = None
    for q in range(1, 5):
        upper = window[32 + 8 * q : 32 + 8 * q + count, :]
        lower = window[32 - 8 * q : 32 - 8 * q + count, :]
        term = stencil_weights[q - 1] * (upper - lower)
        total = term if total is None else total + term
    return window[32 : 32 + count, :] - courant * total


def first_rate_kernel(state, own_product, courant, near_hi, near_lo, partial, product):
    wide = halo * lines
    total = own_product.shape[0]
    speed = courant[...]
    for at in range(0, total + 128, 64):
        partial[at : at + 64, :] = azimuth(state, speed, at, 64)
    product[64 : 64 + total, :] = own_product[...]
    rows = jnp.concatenate([state[32:wide, :], state[wide + total : wide + total + 64, :]], axis=0)
    hi, lo = halves(rows)
    both = near_product(hi, lo, near_hi[...], near_lo[...])
    product[:64, :] = both[:64]
    product[64 + total :, :] = both[64:]


def rate_kernel(old, new, field_at, state, field, courant, near_hi, near_lo, partial, product):
    speed = courant[...]
    count = partial.shape[0]
    step = 64
    for at in range(0, count, step):
        ahead = azimuth(state, speed, at, step)
        partial[at : at + step, :] = old * field[field_at + at : field_at + at + step, :] + new * ahead
    chunk = count // 4 if count % 64 == 0 and count // 4 % 16 == 0 else 64
    for at in range(0, count, chunk):
        hi, lo = halves(state[32 + at : 32 + at + chunk, :])
        product[at : at + chunk, :] = new * near_product(hi, lo, near_hi[...], near_lo[...])


def opposite_stack(proj, new):
    value = proj if new is None else new * proj
    hi = value.astype(bf16).astype(f32)
    lo = value - hi
    return jnp.concatenate([hi, lo, hi, lo], axis=0).astype(bf16).T


def advance(at, step, stack_rows, state, partial, product, right_all):
    far = dot(stack_rows, right_all)
    return partial[at : at + step, :] + state[32 + at : 32 + at + step, :] * (
        product[at : at + step, :] + far
    )


def advance_kernel(new, offset, ordered, opposite, state, partial, product, right_all, left_both, ahead, proj):
    stack = opposite_stack(opposite[...], new)
    if not ordered:
        stack = jnp.concatenate([stack[-128:-64], stack[:-128], stack[-64:]], axis=0)
    step = 64
    count = ahead.shape[0]
    for at in range(0, count, step):
        rows = advance(at, step, stack[at : at + step], state, partial, product, right_all[...])
        ahead[at : at + step, :] = rows
    inner = proj.shape[1]
    hi, lo = halves(ahead[32 : 32 + inner, :])
    proj[...] = projected(hi, lo, left_both[...])


def last_kernel(new, opposite, state, partial, product, right_all, out):
    stack = opposite_stack(opposite[...], new)
    for at in range(0, 512, 64):
        rows = advance(at, 64, stack[at : at + 64], state, partial, product, right_all[...])
        out[:, at // 8 : at // 8 + 8, :] = jnp.swapaxes(rows.reshape(8, lines, -1), 0, 1)


def on_chip(count):
    return [pl.BlockSpec(memory_space=pltpu.VMEM)] * count


def run(kernel, outs, *args, scalars=0, name):
    single = not isinstance(outs[0], tuple)
    shapes = [outs] if single else outs
    specs = [pl.BlockSpec(memory_space=pltpu.SMEM)] * scalars + on_chip(len(args) - scalars)
    result = pl.pallas_call(
        kernel,
        out_shape=[jax.ShapeDtypeStruct(s, f32) for s in shapes],
        in_specs=specs,
        out_specs=on_chip(len(shapes)),
        compiler_params=pltpu.CompilerParams(vmem_limit_bytes=16 << 20),
        name=name,
    )(*args)
    return result[0] if single else result


def body(field, courant):
    count = field.shape[2]
    cells = field.shape[1] * lines
    size = lax.axis_size("theta")
    opposite = [(i, (i + size // 2) % size) for i in range(size)]
    pair = [(i, i ^ 1) for i in range(size)]
    other = [(i, (i + 1 if i % 2 else i - 1) % size) for i in range(size)]
    near_hi, near_lo, left_both, right_all = (jnp.asarray(t) for t in tables(count))
    par = (lax.axis_index("theta") % 2).astype(jnp.int32).reshape(1)
    speed = courant.reshape(1, count)
    edge = (halo * lines, count)

    to_pair, to_other = run(edges_kernel, [edge, edge], par, field, scalars=1, name="edges")
    from_pair = lax.ppermute(to_pair, "theta", pair)
    from_other = lax.ppermute(to_other, "theta", other)
    own, own_product, own_proj = run(
        own_kernel, [(cells, count), (cells, count), (rank, cells)],
        field, near_hi, near_lo, left_both, name="own",
    )
    start, proj = run(
        join_kernel, [(cells + 192, count), (rank, cells + 128)],
        par, own, own_proj, from_pair, from_other, left_both, scalars=1, name="join",
    )
    proj = lax.ppermute(proj, "theta", opposite)
    partial, product = run(
        first_rate_kernel, [(cells + 128, count), (cells + 128, count)],
        start, own_product, speed, near_hi, near_lo, name="rate1",
    )
    first, proj = run(
        functools.partial(advance_kernel, None, 32, False),
        [(cells + 128, count), (rank, cells + 64)],
        proj, start, partial, product, right_all, left_both, name="advance1",
    )
    proj = lax.ppermute(proj, "theta", opposite)
    partial, product = run(
        functools.partial(rate_kernel, 0.75, 0.25, 64), [(cells + 64, count), (cells + 64, count)],
        first, start, speed, near_hi, near_lo, name="rate2",
    )
    second, proj = run(
        functools.partial(advance_kernel, 0.25, 32, True), [(cells + 64, count), (rank, cells)],
        proj, first, partial, product, right_all, left_both, name="advance2",
    )
    proj = lax.ppermute(proj, "theta", opposite)
    partial, product = run(
        functools.partial(rate_kernel, 1.0 / 3.0, 2.0 / 3.0, 96), [(cells, count), (cells, count)],
        second, start, speed, near_hi, near_lo, name="rate3",
    )
    return run(
        functools.partial(last_kernel, 2.0 / 3.0), field.shape,
        proj, second, partial, product, right_all, name="advance3",
    )


def solution(mesh):
    placed = (P("gz", "theta", None), P())
    return jax.shard_map(
        body, mesh=mesh, in_specs=placed, out_specs=P("gz", "theta", None), check_vma=False
    )
```

profile of v0, /device:TPU:8, one launch (start us, length us, event | category | flops | bytes accessed | tf_op | source)
XLA Modules:
  0.0 46.7 jit_solution(15298261647815958418)
XLA Ops:
  0.0 0.0 copy-start
  0.0 0.0 copy-start.3
  0.0 1.7 %copy-done.3 = f32[8,64,1024]{2,1,0:T(8,128)S(1)} copy-done((f32[8,64,1024]{2,1,0:T(8,128)S(1)}, f32[8,64,1024]{2,1,0:T(8,128)}, u32[]{:S(2)}) %copy-start.3) | copy-done | bytes 2097176
  1.7 0.2 edges.1
  1.9 0.1 collective-permute-start
  2.0 9.9 %collective-permute-start.1 = (f32[96,1024]{1,0:T(8,128)S(1)}, f32[96,1024]{1,0:T(8,128)S(1)}, u32[]{:S(2)}, u32[]{:S(2)}) collective-permute-start(f32[96,1024]{1,0:T(8,128)S(1)} %get-tuple-element.25), channel_id=1, source_target_pairs={{0,254},{2,4},{4,2},{6,8},{8,6},{10,12},{12,10},{14,16},{16,14},{1... | collective-permute-start | bytes 1179656 | tf_op jit(solution)/shard_map/ppermute | solution.py:239
  11.9 0.0 copy-done
  11.9 0.0 copy-start.1
  11.9 1.6 %copy-done.1 = bf16[1024,1024]{1,0:T(8,128)(2,1)S(1)} copy-done((bf16[1024,1024]{1,0:T(8,128)(2,1)S(1)}, bf16[1024,1024]{1,0:T(8,128)(2,1)}, u32[]{:S(2)}) %copy-start.1) | copy-done | bytes 2097176
  13.5 0.0 copy-start.4
  13.5 0.9 %copy-done.4 = bf16[1024,128]{1,0:T(8,128)(2,1)S(1)} copy-done((bf16[1024,128]{1,0:T(8,128)(2,1)S(1)}, bf16[1024,128]{1,0:T(8,128)(2,1)}, u32[]{:S(2)}) %copy-start.4) | copy-done | bytes 262168
  14.5 4.3 %own.1 = (f32[512,1024]{1,0:T(8,128)S(1)}, f32[512,1024]{1,0:T(8,128)S(1)}, f32[24,512]{1,0:T(8,128)S(1)}) custom-call(f32[8,64,1024]{2,1,0:T(8,128)S(1)} %copy-done.3, bf16[1024,1024]{1,0:T(8,128)(2,1)S(1)} %copy-done.1, bf16[1024,1024]{1,0:T(8,128)(2,1)S(1)} %copy-done, bf16[1024,128]{1,0:T(8,128)(2,1)S(1)} %copy-done.4), custom_call_target="tpu_custom_call" | custom-call | tf_op jit(solution)/shard_map/own/pallas_call | solution.py:214
  18.8 0.0 copy-start.2
  18.8 0.0 copy-start.7
  18.8 0.0 collective-permute-done.from_pair
  18.8 0.0 collective-permute-done.1.from_other
  18.8 0.5 %join.1 = (f32[704,1024]{1,0:T(8,128)S(1)}, f32[24,640]{1,0:T(8,128)S(1)}) custom-call(s32[1]{0:T(128)} %bitcast.par, f32[512,1024]{1,0:T(8,128)S(1)} %get-tuple-element.22.own, f32[24,512]{1,0:T(8,128)S(1)} %get-tuple-element.23.proj_own, f32[96,1024]{1,0:T(8,128)S(1)} %collective-permute-done.from_pair, f32[96,1024]{1,0:T(8,128)S(1)} %collective-permute-done.1.from_other, ...), custom_call_target="tpu_custom_call" | custom-call | tf_op jit(solution)/shard_map/join/pallas_call | solution.py:214
  19.3 1.3 %collective-permute-start.2 = (f32[24,640]{1,0:T(8,128)S(1)}, f32[24,640]{1,0:T(8,128)S(1)}, u32[]{:S(2)}, u32[]{:S(2)}) collective-permute-start(f32[24,640]{1,0:T(8,128)S(1)} %get-tuple-element.26), channel_id=1, source_target_pairs={{0,128},{2,130},{4,132},{6,134},{8,136},{10,138},{12,140},{14,142}... | collective-permute-start | bytes 184328 | tf_op jit(solution)/shard_map/ppermute | solution.py:248
  20.6 0.0 copy-done.2
  20.6 0.0 copy-done.7
  20.6 0.0 copy-start.5
  20.6 0.0 copy-start.6
  20.7 3.5 %rate1.1 = (f32[640,1024]{1,0:T(8,128)S(1)}, f32[640,1024]{1,0:T(8,128)S(1)}) custom-call(f32[704,1024]{1,0:T(8,128)S(1)} %get-tuple-element.27.state.field, f32[512,1024]{1,0:T(8,128)S(1)} %get-tuple-element.28.own_product, f32[1,1024]{1,0:T(1,128)S(1)} %bitcast.2, bf16[1024,1024]{1,0:T(8,128)(2,1)S(1)} %copy-done.2, bf16[1024,1024]{1,0:T(8,128)(2,1)S(1)} %copy-done), custom_call_target="tpu_custom_call" | custom-call | tf_op jit(solution)/shard_map/rate1/pallas_call | solution.py:214
  24.2 0.9 %collective-permute-done.2.opposite = f32[24,640]{1,0:T(8,128)S(1)} collective-permute-done((f32[24,640]{1,0:T(8,128)S(1)}, f32[24,640]{1,0:T(8,128)S(1)}, u32[]{:S(2)}, u32[]{:S(2)}) %collective-permute-start.2) | collective-permute-done | bytes 61472 | tf_op jit(solution)/shard_map/ppermute | solution.py:248
  25.1 0.0 copy-done.5
  25.1 0.0 copy-done.6
  25.1 1.6 %advance1.1 = (f32[640,1024]{1,0:T(8,128)S(1)}, f32[24,576]{1,0:T(8,128)S(1)}) custom-call(f32[24,640]{1,0:T(8,128)S(1)} %collective-permute-done.2.opposite, f32[704,1024]{1,0:T(8,128)S(1)} %get-tuple-element.27.state.field, f32[640,1024]{1,0:T(8,128)S(1)} %get-tuple-element.29.partial, f32[640,1024]{1,0:T(8,128)S(1)} %get-tuple-element.30.product, ...), custom_call_target="tpu_custom_call" | custom-call | tf_op jit(solution)/shard_map/advance1/pallas_call | solution.py:214
  26.7 1.6 %collective-permute-start.3 = (f32[24,576]{1,0:T(8,128)S(1)}, f32[24,576]{1,0:T(8,128)S(1)}, u32[]{:S(2)}, u32[]{:S(2)}) collective-permute-start(f32[24,576]{1,0:T(8,128)S(1)} %get-tuple-element.31), channel_id=1, source_target_pairs={{0,128},{2,130},{4,132},{6,134},{8,136},{10,138},{12,140},{14,142}... | collective-permute-start | bytes 165896 | tf_op jit(solution)/shard_map/ppermute | solution.py:258
  28.4 6.4 %rate2.1 = (f32[576,1024]{1,0:T(8,128)S(1)}, f32[576,1024]{1,0:T(8,128)S(1)}) custom-call(f32[640,1024]{1,0:T(8,128)S(1)} %get-tuple-element.32.state, f32[704,1024]{1,0:T(8,128)S(1)} %get-tuple-element.27.state.field, f32[1,1024]{1,0:T(1,128)S(1)} %bitcast.3, bf16[1024,1024]{1,0:T(8,128)(2,1)S(1)} %copy-done.2, bf16[1024,1024]{1,0:T(8,128)(2,1)S(1)} %copy-done), custom_call_target="tpu_custom_call" | custom-call | tf_op jit(solution)/shard_map/rate2/pallas_call | solution.py:214
  34.7 0.0 collective-permute-done.3.opposite
  34.7 1.4 %advance2.1 = (f32[576,1024]{1,0:T(8,128)S(1)}, f32[24,512]{1,0:T(8,128)S(1)}) custom-call(f32[24,576]{1,0:T(8,128)S(1)} %collective-permute-done.3.opposite, f32[640,1024]{1,0:T(8,128)S(1)} %get-tuple-element.32.state, f32[576,1024]{1,0:T(8,128)S(1)} %get-tuple-element.33.partial, f32[576,1024]{1,0:T(8,128)S(1)} %get-tuple-element.34.product, ...), custom_call_target="tpu_custom_call" | custom-call | tf_op jit(solution)/shard_map/advance2/pallas_call | solution.py:214
  36.2 2.5 %collective-permute-start.4 = (f32[24,512]{1,0:T(8,128)S(1)}, f32[24,512]{1,0:T(8,128)S(1)}, u32[]{:S(2)}, u32[]{:S(2)}) collective-permute-start(f32[24,512]{1,0:T(8,128)S(1)} %get-tuple-element.35), channel_id=1, source_target_pairs={{0,128},{2,130},{4,132},{6,134},{8,136},{10,138},{12,140},{14,142}... | collective-permute-start | bytes 147464 | tf_op jit(solution)/shard_map/ppermute | solution.py:267
  38.6 5.7 %rate3.1 = (f32[512,1024]{1,0:T(8,128)S(1)}, f32[512,1024]{1,0:T(8,128)S(1)}) custom-call(f32[576,1024]{1,0:T(8,128)S(1)} %get-tuple-element.36.state, f32[704,1024]{1,0:T(8,128)S(1)} %get-tuple-element.27.state.field, f32[1,1024]{1,0:T(1,128)S(1)} %bitcast.4, bf16[1024,1024]{1,0:T(8,128)(2,1)S(1)} %copy-done.2, bf16[1024,1024]{1,0:T(8,128)(2,1)S(1)} %copy-done), custom_call_target="tpu_custom_call" | custom-call | tf_op jit(solution)/shard_map/rate3/pallas_call | solution.py:214
  44.3 0.0 collective-permute-done.4.opposite
  44.3 2.4 %advance3.1 = f32[8,64,1024]{2,1,0:T(8,128)} custom-call(f32[24,512]{1,0:T(8,128)S(1)} %collective-permute-done.4.opposite, f32[576,1024]{1,0:T(8,128)S(1)} %get-tuple-element.36.state, f32[512,1024]{1,0:T(8,128)S(1)} %get-tuple-element.37.partial, f32[512,1024]{1,0:T(8,128)S(1)} %get-tuple-element.38.product, bf16[96,1024]{1,0:T(8,128)(2,1)S(1)} %copy-done.6), custom_call_target="tpu_custom_call" | custom-call | tf_op jit(solution)/shard_map/advance3/pallas_call | solution.py:214
Async XLA Ops:
  0.0 11.9 %copy-start = (bf16[1024,1024]{1,0:T(8,128)(2,1)S(1)}, bf16[1024,1024]{1,0:T(8,128)(2,1)}, u32[]{:S(2)}) copy-start(bf16[1024,1024]{1,0:T(8,128)(2,1)} %constant.28.clone.near_lo) | copy-start | bytes 6291460
  0.0 1.7 %copy-start.3 = (f32[8,64,1024]{2,1,0:T(8,128)S(1)}, f32[8,64,1024]{2,1,0:T(8,128)}, u32[]{:S(2)}) copy-start(f32[8,64,1024]{2,1,0:T(8,128)} %field.3) | copy-start | bytes 6291460
  1.9 16.9 %collective-permute-start = (f32[96,1024]{1,0:T(8,128)S(1)}, f32[96,1024]{1,0:T(8,128)S(1)}, u32[]{:S(2)}, u32[]{:S(2)}) collective-permute-start(f32[96,1024]{1,0:T(8,128)S(1)} %get-tuple-element.24), channel_id=1, source_target_pairs={{0,2},{2,0},{4,6},{6,4},{8,10},{10,8},{12,14},{14,12},{16,18},{18,... | collective-permute-start | bytes 1179656 | tf_op jit(solution)/shard_map/ppermute | solution.py:238
  2.0 16.8 %collective-permute-start.1 = (f32[96,1024]{1,0:T(8,128)S(1)}, f32[96,1024]{1,0:T(8,128)S(1)}, u32[]{:S(2)}, u32[]{:S(2)}) collective-permute-start(f32[96,1024]{1,0:T(8,128)S(1)} %get-tuple-element.25), channel_id=1, source_target_pairs={{0,254},{2,4},{4,2},{6,8},{8,6},{10,12},{12,10},{14,16},{16,14},{1... | collective-permute-start | bytes 1179656 | tf_op jit(solution)/shard_map/ppermute | solution.py:239
  11.9 1.6 %copy-start.1 = (bf16[1024,1024]{1,0:T(8,128)(2,1)S(1)}, bf16[1024,1024]{1,0:T(8,128)(2,1)}, u32[]{:S(2)}) copy-start(bf16[1024,1024]{1,0:T(8,128)(2,1)} %constant.27.clone.near_hi) | copy-start | bytes 6291460
  13.5 0.9 %copy-start.4 = (bf16[1024,128]{1,0:T(8,128)(2,1)S(1)}, bf16[1024,128]{1,0:T(8,128)(2,1)}, u32[]{:S(2)}) copy-start(bf16[1024,128]{1,0:T(8,128)(2,1)} %constant.29.clone.left_both) | copy-start | bytes 786436
  18.8 1.9 %copy-start.2 = (bf16[1024,1024]{1,0:T(8,128)(2,1)S(1)}, bf16[1024,1024]{1,0:T(8,128)(2,1)}, u32[]{:S(2)}) copy-start(bf16[1024,1024]{1,0:T(8,128)(2,1)} %constant.27.clone.near_hi) | copy-start | bytes 6291460
  18.8 1.9 %copy-start.7 = (f32[1024]{0:T(1024)S(1)}, f32[1024]{0:T(1024)}, u32[]{:S(2)}) copy-start(f32[1024]{0:T(1024)} %param.7) | copy-start | bytes 12292
  19.3 5.8 %collective-permute-start.2 = (f32[24,640]{1,0:T(8,128)S(1)}, f32[24,640]{1,0:T(8,128)S(1)}, u32[]{:S(2)}, u32[]{:S(2)}) collective-permute-start(f32[24,640]{1,0:T(8,128)S(1)} %get-tuple-element.26), channel_id=1, source_target_pairs={{0,128},{2,130},{4,132},{6,134},{8,136},{10,138},{12,140},{14,142}... | collective-permute-start | bytes 184328 | tf_op jit(solution)/shard_map/ppermute | solution.py:248
  20.6 4.5 %copy-start.5 = (bf16[1024,128]{1,0:T(8,128)(2,1)S(1)}, bf16[1024,128]{1,0:T(8,128)(2,1)}, u32[]{:S(2)}) copy-start(bf16[1024,128]{1,0:T(8,128)(2,1)} %constant.29.clone.left_both) | copy-start | bytes 786436
  20.6 4.5 %copy-start.6 = (bf16[96,1024]{1,0:T(8,128)(2,1)S(1)}, bf16[96,1024]{1,0:T(8,128)(2,1)}, u32[]{:S(2)}) copy-start(bf16[96,1024]{1,0:T(8,128)(2,1)} %constant.30.clone.right_all) | copy-start | bytes 589828
  26.7 8.0 %collective-permute-start.3 = (f32[24,576]{1,0:T(8,128)S(1)}, f32[24,576]{1,0:T(8,128)S(1)}, u32[]{:S(2)}, u32[]{:S(2)}) collective-permute-start(f32[24,576]{1,0:T(8,128)S(1)} %get-tuple-element.31), channel_id=1, source_target_pairs={{0,128},{2,130},{4,132},{6,134},{8,136},{10,138},{12,140},{14,142}... | collective-permute-start | bytes 165896 | tf_op jit(solution)/shard_map/ppermute | solution.py:258
  36.2 8.1 %collective-permute-start.4 = (f32[24,512]{1,0:T(8,128)S(1)}, f32[24,512]{1,0:T(8,128)S(1)}, u32[]{:S(2)}, u32[]{:S(2)}) collective-permute-start(f32[24,512]{1,0:T(8,128)S(1)} %get-tuple-element.35), channel_id=1, source_target_pairs={{0,128},{2,130},{4,132},{6,134},{8,136},{10,138},{12,140},{14,142}... | collective-permute-start | bytes 147464 | tf_op jit(solution)/shard_map/ppermute | solution.py:267
where the time goes:
time: 46.8 us; the launch traced here: 46.7 us
  Pallas kernels  26 us (56%)
  starting transfers between devices  15.4 us (33%)
  local copies, waits for them, and re-layouts  4.3 us (9%)
  waiting for transfers between devices  0.96 us (2%)
    pallas_call x9, Pallas kernels, run(): pl.pallas_call(kernel, out_shape=[jax.ShapeDtypeStruct(s, f32) for s in s...  26 us
    ppermute x1, starting transfers between devices, body(): from_other = lax.ppermute(to_other, 'theta', other)  9.88 us
    ppermute x3, starting transfers between devices, body(): proj = lax.ppermute(proj, 'theta', opposite)  5.38 us
    unnamed x16, local copies, waits for them, and re-layouts  4.3 us
    ppermute x3, waiting for transfers between devices, body(): proj = lax.ppermute(proj, 'theta', opposite)  0.95 us
  transfers between devices with their start and end apart: 5, of which 1 were waited for; matrix products, arithmetic and copies ran while one was open for 0% of the time, Pallas kernels for 43%

commit v1 on v0

v1 whole, which is shorter than its diff:
```python
import functools
import math

import jax
import jax.numpy as jnp
import ml_dtypes
import numpy as np
from jax import lax
from jax.experimental import pallas as pl
from jax.experimental.pallas import tpu as pltpu
from jax.sharding import PartitionSpec as P

stencil_weights = (4.0 / 5.0, -1.0 / 5.0, 4.0 / 105.0, -1.0 / 280.0)
radial_step = 0.2
rank = 24
block_rank = 20
tile = 256
lines = 8
halo = 12
f32 = jnp.float32
bf16 = jnp.bfloat16


def split_table(a):
    hi = a.astype(ml_dtypes.bfloat16)
    lo = (a - hi.astype(np.float64)).astype(ml_dtypes.bfloat16)
    return hi, lo


def cross_factors(block, terms):
    rest = block.copy()
    left, right = [], []
    for _ in range(terms):
        at = np.unravel_index(np.argmax(np.abs(rest)), rest.shape)
        column = rest[:, at[1]] / rest[at]
        row = rest[at[0], :].copy()
        left.append(column)
        right.append(row)
        rest = rest - column[:, None] * row[None, :]
    return np.stack(left, axis=1), np.stack(right, axis=0)


@functools.lru_cache(maxsize=None)
def tables(count):
    intervals = 2 * count - 1
    row = np.arange(count)[:, None]
    col = np.arange(2 * count)[None, :]
    sines = np.array([math.sin(math.pi * k / (2 * intervals)) for k in range(3 * count)])
    same = row == col
    spacing = -2.0 * sines[row + col] * np.sign(row - col) * sines[np.abs(row - col)]
    row_factor = np.where(row == 0, 2.0, 1.0)
    col_factor = np.where((col == 0) | (col == intervals), 2.0, 1.0)
    parity = np.where((row + col) % 2 == 0, 1.0, -1.0)
    off = np.where(same, 0.0, row_factor / col_factor * parity / np.where(same, 1.0, spacing))
    matrix = off - np.where(same, off.sum(axis=1, keepdims=True), 0.0)
    near = matrix[:, :count].T
    far = matrix[:, count:][:, ::-1].T
    scale = -(radial_step / intervals) * sines[2 * np.arange(count)] ** 2
    half = count // 2
    left = np.zeros((count, 64))
    across = np.zeros((64, count))
    left[:, :rank], right = cross_factors(far, rank)
    other = slice(rank, rank + block_rank)
    sibling = slice(rank + block_rank, rank + 2 * block_rank)
    for span, columns in ((half, other), (tile, sibling)):
        for at in range(0, count, span):
            to = at + span if (at // span) % 2 == 0 else at - span
            block = near[at : at + span, to : to + span]
            left[at : at + span, columns], across[columns, to : to + span] = cross_factors(
                block, block_rank
            )
    diagonal = np.concatenate(
        [near[at : at + tile, at : at + tile] for at in range(0, count, tile)], axis=1
    )
    diagonal_hi, diagonal_lo = split_table(diagonal * scale[None, :])
    across_hi, across_lo = split_table(across * scale[None, :])
    near_all = np.concatenate([diagonal_hi, diagonal_hi, diagonal_lo] + 4 * [across_hi] + 2 * [across_lo])
    left_both = np.concatenate(split_table(left), axis=1)
    right_hi, right_lo = split_table(right * scale[None, :])
    right_all = np.concatenate([right_hi, right_hi, right_lo, right_lo])
    return near_all, left_both, right_all


def halves(x):
    hi = x.astype(bf16)
    lo = (x - hi.astype(f32)).astype(bf16)
    return hi, lo


def dot(a, b):
    return jnp.dot(a, b, preferred_element_type=f32)


def columns_of(at, width=tile):
    return slice(at * width, (at + 1) * width)


def projected(hi, lo, left):
    parts = []
    for t in range(hi.shape[1] // tile):
        rows = columns_of(t)
        parts.append(dot(hi[:, rows], left[rows, :]) + dot(lo[:, rows], left[rows, :]))
    return parts


def far_values(parts):
    both = functools.reduce(jnp.add, parts).T
    return both[:rank] + both[64 : 64 + rank]


def near_tile(t, hi, lo, parts, near):
    place = lax.broadcasted_iota(jnp.int32, parts[0].shape, 1) % 64
    halves_sum = parts[2] + parts[3] if t < 2 else parts[0] + parts[1]
    values = jnp.where(place < rank + block_rank, halves_sum, parts[t ^ 1])
    value_hi, value_lo = halves(values)
    cols = columns_of(t)
    left = jnp.concatenate([hi[:, cols], lo[:, cols], hi[:, cols], value_hi, value_lo, value_hi], axis=1)
    return dot(left, near[:, cols])


def azimuth(state, courant, start, cells, lane):
    cols = columns_of(lane, 128)
    count = cells * lines
    window = state[start : start + count + 64, cols]
    total = None
    for q in range(1, 5):
        upper = window[32 + 8 * q : 32 + 8 * q + count, :]
        lower = window[32 - 8 * q : 32 - 8 * q + count, :]
        term = stencil_weights[q - 1] * (upper - lower)
        total = term if total is None else total + term
    return window[32 : 32 + count, :] - courant[:, cols] * total


def fetch(pairs, sems):
    copies = [pltpu.make_async_copy(source, target, sems.at[i]) for i, (source, target) in enumerate(pairs)]
    for copy in copies:
        copy.start()
    return copies


def await_all(copies):
    for copy in copies:
        copy.wait()


def own_section(wedge, near, left, state, product, proj):
    for at in range(0, 64, 16):
        rows = jnp.swapaxes(wedge[:, at : at + 16, :], 0, 1).reshape(16 * lines, -1)
        state[at * lines : (at + 16) * lines, :] = rows
    hi, lo = halves(state[...])
    parts = projected(hi, lo, left)
    proj[...] = far_values(parts)
    for t in range(4):
        product[:, columns_of(t)] = near_tile(t, hi, lo, parts, near)


def ends_kernel(place, to_pair, to_other, left, proj_pair, proj_other, rows):
    @pl.when(place[0] == 0)
    def _():
        rows[:64, :] = to_pair[32:, :]
        rows[64:, :] = to_other[:64, :]

    @pl.when(place[0] != 0)
    def _():
        rows[:64, :] = to_pair[:64, :]
        rows[64:, :] = to_other[32:, :]

    hi, lo = halves(rows[...])
    values = far_values(projected(hi, lo, left))
    proj_pair[...] = values[:, :64]
    proj_other[...] = values[:, 64:]


def inside_kernel(state, courant, partial):
    for lane in range(8):
        for at in range(0, 448, 112):
            partial[at : at + 112, columns_of(lane, 128)] = azimuth(state, courant, at, 14, lane)


def launch_kernel(place, field, near, left, to_pair, to_other, *refs):
    outs, (wedge, *here, sems) = refs[:3], refs[3:]
    first, middle, last = slice(0, 16), slice(16, 48), slice(48, 64)
    edges = fetch([(field.at[:, span, :], wedge.at[:, span, :]) for span in (first, last)], sems)

    def others():
        return [(field.at[:, middle, :], wedge.at[:, middle, :])] + list(zip((near, left), here))

    @pl.when(place[1] != 0)
    def _():
        fetch(others(), sems.at[2:])

    await_all(edges)
    low = jnp.swapaxes(wedge[:, first, :], 0, 1)[:halo].reshape(halo * lines, -1)
    high = jnp.swapaxes(wedge[:, last, :], 0, 1)[16 - halo :].reshape(halo * lines, -1)

    @pl.when(place[0] == 0)
    def _():
        to_pair[...] = high
        to_other[...] = low

    @pl.when(place[0] != 0)
    def _():
        to_pair[...] = low
        to_other[...] = high

    @pl.when(place[1] != 0)
    def _():
        await_all([pltpu.make_async_copy(*ends, sems.at[2 + i]) for i, ends in enumerate(others())])
        own_section(wedge, *here, *outs)


def own_kernel(place, field, near, left, *refs):
    done, outs, (wedge, *here, sems) = refs[:3], refs[3:6], refs[6:]

    @pl.when(place[1] == 0)
    def _():
        await_all(fetch([(field, wedge)] + list(zip((near, left), here)), sems))
        own_section(wedge, *here, *outs)

    @pl.when(place[1] != 0)
    def _():
        for out, ready in zip(outs, done):
            out[...] = ready[...]


def join_kernel(place, from_pair, from_other, own, courant, near, left, sides, partial, product):
    wide = halo * lines
    sides[0, wide:, :] = own[:64, :]
    sides[1, :64, :] = own[448:, :]

    @pl.when(place[0] == 0)
    def _():
        sides[0, :wide, :] = from_other[...]
        sides[1, 64:, :] = from_pair[...]

    @pl.when(place[0] != 0)
    def _():
        sides[0, :wide, :] = from_pair[...]
        sides[1, 64:, :] = from_other[...]

    rows = jnp.concatenate([sides[0, 32:wide, :], sides[1, 64:128, :]], axis=0)
    hi, lo = halves(rows)
    parts = projected(hi, lo, left)
    for t in range(4):
        both = near_tile(t, hi, lo, parts, near)
        product[0, :, columns_of(t)] = both[:64]
        product[1, :, columns_of(t)] = both[64:]
    for lane in range(8):
        for side in range(2):
            partial[side, :, columns_of(lane, 128)] = azimuth(sides.at[side], courant, 0, 12, lane)


def rate_kernel(old, new, cells, state, hi, lo, parts, own, sides, courant, near, partial, product):
    count = partial.shape[0]
    extra = (count - own.shape[0]) // 2
    pieces = [parts[:, columns_of(t, 128)] for t in range(4)]
    for t in range(4):
        product[:, columns_of(t)] = new * near_tile(t, hi, lo, pieces, near)
        for lane in (2 * t, 2 * t + 1):
            cols = columns_of(lane, 128)
            for at in range(0, count, cells * lines):
                end = at + cells * lines
                field = own[max(at - extra, 0) : min(end - extra, own.shape[0]), cols]
                if at < extra:
                    field = jnp.concatenate([sides[0, 96 - extra : 96, cols], field], axis=0)
                if end > count - extra:
                    field = jnp.concatenate([field, sides[1, 64 : 64 + extra, cols]], axis=0)
                ahead = azimuth(state, courant, at, cells, lane)
                partial[at:end, cols] = old * field + new * ahead


def opposite_stack(proj, new):
    value = new * proj
    hi = value.astype(bf16).astype(f32)
    lo = value - hi
    return jnp.concatenate([hi, lo, hi, lo], axis=0).astype(bf16).T


def advanced_rows(partial, state, product, stack_rows, right):
    return partial + state * (product + dot(stack_rows, right[...]))


def finish(ahead, left, hi_out, lo_out, parts_out, proj):
    inner = proj.shape[1]
    hi, lo = halves(ahead[32 : 32 + inner, :])
    hi_out[...] = hi
    lo_out[...] = lo
    parts = projected(hi, lo, left)
    for t in range(4):
        parts_out[:, columns_of(t, 128)] = parts[t]
    proj[...] = far_values(parts)


def first_kernel(place, opposite, by_other, by_pair, own, partial, product, sides, side_partial, side_product,
                 right, left, ahead, hi, lo, parts, proj, ends):
    near_pair = opposite_stack(by_pair[...], 1.0)
    near_other = opposite_stack(by_other[...], 1.0)

    @pl.when(place[0] == 0)
    def _():
        ends[0] = near_other
        ends[1] = near_pair

    @pl.when(place[0] != 0)
    def _():
        ends[0] = near_pair
        ends[1] = near_other

    stack = opposite_stack(opposite[...], 1.0)
    ahead[:64, :] = advanced_rows(side_partial[0, :64], sides[0, 32:96], side_product[0], ends[0], right)
    ahead[576:, :] = advanced_rows(side_partial[1, 32:], sides[1, 64:128], side_product[1], ends[1], right)
    low = side_partial[0, 64:]
    high = side_partial[1, :32]
    for at in range(0, 512, 128):
        inside = partial[max(at - 32, 0) : min(at + 96, 448)]
        if at == 0:
            inside = jnp.concatenate([low, inside], axis=0)
        if at == 384:
            inside = jnp.concatenate([inside, high], axis=0)
        rows = slice(at, at + 128)
        ahead[64 + at : 192 + at, :] = advanced_rows(inside, own[rows], product[rows], stack[rows], right)
    finish(ahead, left, hi, lo, parts, proj)


def second_kernel(new, opposite, state, partial, product, right, left, ahead, hi, lo, parts, proj):
    stack = opposite_stack(opposite[...], new)
    step = 144
    for at in range(0, ahead.shape[0], step):
        rows = slice(at, at + step)
        ahead[rows, :] = advanced_rows(
            partial[rows], state[32 + at : 32 + at + step], product[rows], stack[rows], right
        )
    finish(ahead, left, hi, lo, parts, proj)


def last_kernel(new, opposite, state, partial, product, right, out):
    stack = opposite_stack(opposite[...], new)
    for at in range(0, 512, 64):
        rows = slice(at, at + 64)
        done = advanced_rows(partial[rows], state[32 + at : 96 + at], product[rows], stack[rows], right)
        out[:, at // 8 : at // 8 + 8, :] = jnp.swapaxes(done.reshape(8, lines, -1), 0, 1)


def shape_of(*dims, dtype=f32):
    return jax.ShapeDtypeStruct(dims, dtype)


def run(kernel, outs, *args, name, flops, scalars=0, away=(), scratch=()):
    spaces = [pltpu.SMEM if i < scalars else pltpu.HBM if i in away else pltpu.VMEM for i in range(len(args))]
    return pl.pallas_call(
        kernel,
        out_shape=outs,
        in_specs=[pl.BlockSpec(memory_space=space) for space in spaces],
        out_specs=jax.tree.map(lambda _: pl.BlockSpec(memory_space=pltpu.VMEM), outs),
        scratch_shapes=scratch,
        compiler_params=pltpu.CompilerParams(vmem_limit_bytes=16 << 20),
        cost_estimate=pl.CostEstimate(flops=flops, transcendentals=0, bytes_accessed=0),
        name=name,
    )(*args)


def body(field, courant):
    count = field.shape[2]
    cells = field.shape[1] * lines
    size = lax.axis_size("theta")
    half = size // 2
    opposite = [(i, (i + half) % size) for i in range(size)]
    pair = [(i, i ^ 1) for i in range(size)]
    other = [(i, (i + 1 if i % 2 else i - 1) % size) for i in range(size)]
    far_pair = [(i, (i + half + (-1 if i % 2 else 1)) % size) for i in range(size)]
    far_other = [(i, (i + half + (1 if i % 2 else -1)) % size) for i in range(size)]
    near, left, right = (jnp.asarray(t) for t in tables(count))
    index = lax.axis_index("theta").astype(jnp.int32)
    place = jnp.stack([index & 1, jnp.where((index & 14) == 14, 0, 1)])
    speed = courant.reshape(1, count)
    edge = shape_of(halo * lines, count)

    own_shapes = [shape_of(cells, count), shape_of(cells, count), shape_of(rank, cells)]
    at_rest = [pltpu.with_memory_space_constraint(a, pltpu.HBM) for a in (field, near, left)]
    room = [pltpu.VMEM(a.shape, a.dtype) for a in at_rest]
    to_pair, to_other, *early = run(
        launch_kernel, [edge, edge] + own_shapes, place, *at_rest, scalars=1, away=(1, 2, 3), name="launch",
        flops=1 << 30, scratch=room + [pltpu.SemaphoreType.DMA((5,))],
    )
    from_pair = lax.ppermute(to_pair, "theta", pair)
    from_other = lax.ppermute(to_other, "theta", other)
    proj_pair, proj_other = run(
        ends_kernel, [shape_of(rank, 64)] * 2, place, to_pair, to_other, left,
        scalars=1, name="ends", flops=0, scratch=[pltpu.VMEM((128, count), f32)],
    )
    by_other = lax.ppermute(proj_other, "theta", far_other)
    by_pair = lax.ppermute(proj_pair, "theta", far_pair)
    own, product, proj = run(
        own_kernel, own_shapes, place, *at_rest, *early, scalars=1, away=(1, 2, 3), name="own",
        flops=4 << 30, scratch=room + [pltpu.SemaphoreType.DMA((3,))],
    )
    proj = lax.ppermute(proj, "theta", opposite)
    partial = run(inside_kernel, shape_of(cells - 64, count), own, speed, name="inside", flops=0)
    sides, side_partial, side_product = run(
        join_kernel, [shape_of(2, 160, count), shape_of(2, 96, count), shape_of(2, 64, count)],
        place, from_pair, from_other, own, speed, near, left, scalars=1, name="join", flops=1 << 30,
    )

    def advanced_shapes(rows):
        inner = rows - 64
        return [shape_of(rows, count), shape_of(inner, count, dtype=bf16), shape_of(inner, count, dtype=bf16),
                shape_of(inner, 512), shape_of(rank, inner)]

    first, hi, lo, parts, proj = run(
        first_kernel, advanced_shapes(cells + 128),
        place, proj, by_other, by_pair, own, partial, product, sides, side_partial, side_product, right, left,
        scalars=1, scratch=[pltpu.VMEM((2, 64, 4 * rank), bf16)], name="advance1", flops=1 << 30,
    )
    proj = lax.ppermute(proj, "theta", opposite)
    partial, product = run(
        functools.partial(rate_kernel, 0.75, 0.25, 12), [shape_of(cells + 64, count)] * 2,
        first, hi, lo, parts, own, sides, speed, near, name="rate2", flops=3 << 30,
    )
    second, hi, lo, parts, proj = run(
        functools.partial(second_kernel, 0.25), advanced_shapes(cells + 64),
        proj, first, partial, product, right, left, name="advance2", flops=1 << 30,
    )
    proj = lax.ppermute(proj, "theta", opposite)
    partial, product = run(
        functools.partial(rate_kernel, 1.0 / 3.0, 2.0 / 3.0, 16), [shape_of(cells, count)] * 2,
        second, hi, lo, parts, own, sides, speed, near, name="rate3", flops=3 << 30,
    )
    return run(
        functools.partial(last_kernel, 2.0 / 3.0), shape_of(*field.shape),
        proj, second, partial, product, right, name="advance3", flops=1 << 30,
    )


def solution(mesh):
    placed = (P("gz", "theta", None), P())
    return jax.shard_map(
        body, mesh=mesh, in_specs=placed, out_specs=P("gz", "theta", None), check_vma=False
    )
```

time: 46.8 us -> 40.2 us (0.86)
  the two profiles are of different devices: /device:TPU:8 before, /device:TPU:230 now
where the time goes in v1:
time: 40.2 us; the launch traced here: 40.1 us
  Pallas kernels  22 us (55%)
  starting transfers between devices  17.8 us (44%)
    pallas_call x10, Pallas kernels, run(): pl.pallas_call(kernel, out_shape=outs, in_specs=[pl.BlockSpec(memory_spac...  22 us
    ppermute x3, starting transfers between devices, body(): proj = lax.ppermute(proj, 'theta', opposite)  9.57 us
    ppermute x1, starting transfers between devices, body(): from_other = lax.ppermute(to_other, 'theta', other)  4.34 us
    ppermute x1, starting transfers between devices, body(): by_other = lax.ppermute(proj_other, 'theta', far_other)  2.69 us
    ppermute x1, starting transfers between devices, body(): by_pair = lax.ppermute(proj_pair, 'theta', far_pair)  1.14 us
  transfers between devices with their start and end apart: 7, of which 0 were waited for; matrix products, arithmetic and copies ran while one was open for 0% of the time, Pallas kernels for 35%

profile of v1, /device:TPU:230, one launch (start us, length us, event | category | flops | bytes accessed | tf_op | source)
XLA Modules:
  0.0 40.1 jit_solution(11938836886212873288)
XLA Ops:
  0.0 0.1 pad_add_fusion.place
  0.1 0.0 copy-start.1
  0.1 2.0 %launch.1 = (f32[96,1024]{1,0:T(8,128)S(1)}, f32[96,1024]{1,0:T(8,128)S(1)}, f32[512,1024]{1,0:T(8,128)S(1)}, f32[512,1024]{1,0:T(8,128)S(1)}, f32[24,512]{1,0:T(8,128)S(1)}) custom-call(s32[2]{0:T(128)S(1)} %pad_add_fusion.place, f32[8,64,1024]{2,1,0:T(8,128)} %field.3, bf16[1152,1024]{1,0:T(8,128)(2,1)} %constant.18.clone.near, ...), custom_call_target="tpu_custom_call" | custom-call | flops 1073741824 | tf_op jit(solution)/shard_map/launch/pallas_call | solution.py:350
  2.1 0.1 collective-permute-start.3
  2.2 4.3 %collective-permute-start.4 = (f32[96,1024]{1,0:T(8,128)S(1)}, f32[96,1024]{1,0:T(8,128)S(1)}, u32[]{:S(2)}, u32[]{:S(2)}) collective-permute-start(f32[96,1024]{1,0:T(8,128)S(1)} %get-tuple-element.37.to_other), channel_id=1, source_target_pairs={{0,254},{2,4},{4,2},{6,8},{8,6},{10,12},{12,10},{14,16},{16,14},{1... | collective-permute-start | bytes 1179656 | tf_op jit(solution)/shard_map/ppermute | solution.py:386
  6.5 0.0 copy-done.1
  6.5 1.0 %ends.1 = (f32[24,64]{1,0:T(8,128)S(1)}, f32[24,64]{1,0:T(8,128)S(1)}) custom-call(s32[2]{0:T(128)S(1)} %pad_add_fusion.place, f32[96,1024]{1,0:T(8,128)S(1)} %get-tuple-element.36.to_pair, f32[96,1024]{1,0:T(8,128)S(1)} %get-tuple-element.37.to_other, bf16[1024,128]{1,0:T(8,128)(2,1)S(1)} %copy-done.1), custom_call_target="tpu_custom_call" | custom-call | tf_op jit(solution)/shard_map/ends/pallas_call | solution.py:350
  7.5 2.7 %collective-permute-start.1 = (f32[24,64]{1,0:T(8,128)S(1)}, f32[24,64]{1,0:T(8,128)S(1)}, u32[]{:S(2)}, u32[]{:S(2)}) collective-permute-start(f32[24,64]{1,0:T(8,128)S(1)} %get-tuple-element.38), channel_id=1, source_target_pairs={{0,126},{2,132},{4,130},{6,136},{8,134},{10,140},{12,138},{14,144}... | collective-permute-start | bytes 18440 | tf_op jit(solution)/shard_map/ppermute | solution.py:391
  10.2 1.1 %collective-permute-start.2 = (f32[24,64]{1,0:T(8,128)S(1)}, f32[24,64]{1,0:T(8,128)S(1)}, u32[]{:S(2)}, u32[]{:S(2)}) collective-permute-start(f32[24,64]{1,0:T(8,128)S(1)} %get-tuple-element.39), channel_id=1, source_target_pairs={{0,130},{2,128},{4,134},{6,132},{8,138},{10,136},{12,142},{14,140}... | collective-permute-start | bytes 18440 | tf_op jit(solution)/shard_map/ppermute | solution.py:392
  11.3 0.0 copy-start.4
  11.3 5.2 %own.1 = (f32[512,1024]{1,0:T(8,128)S(1)}, f32[512,1024]{1,0:T(8,128)S(1)}, f32[24,512]{1,0:T(8,128)S(1)}) custom-call(s32[2]{0:T(128)S(1)} %pad_add_fusion.place, f32[8,64,1024]{2,1,0:T(8,128)} %field.3, bf16[1152,1024]{1,0:T(8,128)(2,1)} %constant.18.clone.near, bf16[1024,128]{1,0:T(8,128)(2,1)} %constant.19.clone.left, ...), custom_call_target="tpu_custom_call" | custom-call | flops 4294967296 | tf_op jit(solution)/shard_map/own/pallas_call | solution.py:350
  16.5 0.0 copy-start
  16.5 0.0 copy-start.2
  16.5 3.3 %collective-permute-start = (f32[24,512]{1,0:T(8,128)S(1)}, f32[24,512]{1,0:T(8,128)S(1)}, u32[]{:S(2)}, u32[]{:S(2)}) collective-permute-start(f32[24,512]{1,0:T(8,128)S(1)} %get-tuple-element.35), channel_id=1, source_target_pairs={{0,128},{2,130},{4,132},{6,134},{8,136},{10,138},{12,140},{14,142}... | collective-permute-start | bytes 147464 | tf_op jit(solution)/shard_map/ppermute | solution.py:397
  19.8 0.0 copy-done.4
  19.8 0.8 %inside.1.partial = f32[448,1024]{1,0:T(8,128)S(1)} custom-call(f32[512,1024]{1,0:T(8,128)S(1)} %get-tuple-element.40.state.own, f32[1,1024]{1,0:T(1,128)S(1)} %bitcast.3), custom_call_target="tpu_custom_call" | custom-call | tf_op jit(solution)/shard_map/inside/pallas_call | solution.py:350
  20.6 0.0 copy-start.3
  20.6 0.0 collective-permute-done.3.from_pair
  20.6 0.0 collective-permute-done.4.from_other
  20.6 0.0 copy-done
  20.7 0.0 copy-done.2
  20.7 1.6 %join.1 = (f32[2,160,1024]{2,1,0:T(8,128)S(1)}, f32[2,96,1024]{2,1,0:T(8,128)S(1)}, f32[2,64,1024]{2,1,0:T(8,128)S(1)}) custom-call(s32[2]{0:T(128)S(1)} %pad_add_fusion.place, f32[96,1024]{1,0:T(8,128)S(1)} %collective-permute-done.3.from_pair, f32[96,1024]{1,0:T(8,128)S(1)} %collective-permute-done.4.from_other, ...), custom_call_target="tpu_custom_call" | custom-call | flops 1073741824 | tf_op jit(solution)/shard_map/join/pallas_call | solution.py:350
  22.3 0.0 collective-permute-done.1.by_other
  22.3 0.0 collective-permute-done.2.by_pair
  22.3 0.0 collective-permute-done.opposite
  22.3 0.0 copy-done.3
  22.3 2.1 %advance1.1 = (f32[640,1024]{1,0:T(8,128)S(1)}, bf16[576,1024]{1,0:T(8,128)(2,1)S(1)}, bf16[576,1024]{1,0:T(8,128)(2,1)S(1)}, f32[576,512]{1,0:T(8,128)S(1)}, f32[24,576]{1,0:T(8,128)S(1)}) custom-call(s32[2]{0:T(128)S(1)} %pad_add_fusion.place, f32[24,512]{1,0:T(8,128)S(1)} %collective-permute-done.opposite, f32[24,64]{1,0:T(8,128)S(1)} %collective-permute-done.1.by_other, ...), custom_call_target="tpu_custom_call" | custom-call | flops 1073741824 | tf_op jit(solution)/shard_map/advance1/pallas_call | solution.py:350
  24.4 3.4 %collective-permute-start.5 = (f32[24,576]{1,0:T(8,128)S(1)}, f32[24,576]{1,0:T(8,128)S(1)}, u32[]{:S(2)}, u32[]{:S(2)}) collective-permute-start(f32[24,576]{1,0:T(8,128)S(1)} %get-tuple-element.45), channel_id=1, source_target_pairs={{0,128},{2,130},{4,132},{6,134},{8,136},{10,138},{12,140},{14,142}... | collective-permute-start | bytes 165896 | tf_op jit(solution)/shard_map/ppermute | solution.py:414
  27.8 2.9 %rate2.1 = (f32[576,1024]{1,0:T(8,128)S(1)}, f32[576,1024]{1,0:T(8,128)S(1)}) custom-call(f32[640,1024]{1,0:T(8,128)S(1)} %get-tuple-element.46.state, bf16[576,1024]{1,0:T(8,128)(2,1)S(1)} %get-tuple-element.47.hi, bf16[576,1024]{1,0:T(8,128)(2,1)S(1)} %get-tuple-element.48.lo, f32[576,512]{1,0:T(8,128)S(1)} %get-tuple-element.49.parts, ...), custom_call_target="tpu_custom_call" | custom-call | flops 3221225472 | tf_op jit(solution)/shard_map/rate2/pallas_call | solution.py:350
  30.7 0.0 collective-permute-done.5.opposite
  30.7 1.4 %advance2.1 = (f32[576,1024]{1,0:T(8,128)S(1)}, bf16[512,1024]{1,0:T(8,128)(2,1)S(1)}, bf16[512,1024]{1,0:T(8,128)(2,1)S(1)}, f32[512,512]{1,0:T(8,128)S(1)}, f32[24,512]{1,0:T(8,128)S(1)}) custom-call(f32[24,576]{1,0:T(8,128)S(1)} %collective-permute-done.5.opposite, f32[640,1024]{1,0:T(8,128)S(1)} %get-tuple-element.46.state, ...), custom_call_target="tpu_custom_call" | custom-call | flops 1073741824 | tf_op jit(solution)/shard_map/advance2/pallas_call | solution.py:350
  32.1 2.9 %collective-permute-start.6 = (f32[24,512]{1,0:T(8,128)S(1)}, f32[24,512]{1,0:T(8,128)S(1)}, u32[]{:S(2)}, u32[]{:S(2)}) collective-permute-start(f32[24,512]{1,0:T(8,128)S(1)} %get-tuple-element.52), channel_id=1, source_target_pairs={{0,128},{2,130},{4,132},{6,134},{8,136},{10,138},{12,140},{14,142}... | collective-permute-start | bytes 147464 | tf_op jit(solution)/shard_map/ppermute | solution.py:423
  35.0 2.8 %rate3.1 = (f32[512,1024]{1,0:T(8,128)S(1)}, f32[512,1024]{1,0:T(8,128)S(1)}) custom-call(f32[576,1024]{1,0:T(8,128)S(1)} %get-tuple-element.53.state, bf16[512,1024]{1,0:T(8,128)(2,1)S(1)} %get-tuple-element.54.hi, bf16[512,1024]{1,0:T(8,128)(2,1)S(1)} %get-tuple-element.55.lo, f32[512,512]{1,0:T(8,128)S(1)} %get-tuple-element.56.parts, ...), custom_call_target="tpu_custom_call" | custom-call | flops 3221225472 | tf_op jit(solution)/shard_map/rate3/pallas_call | solution.py:350
  37.8 0.0 collective-permute-done.6.opposite
  37.8 2.3 %advance3.1 = f32[8,64,1024]{2,1,0:T(8,128)} custom-call(f32[24,512]{1,0:T(8,128)S(1)} %collective-permute-done.6.opposite, f32[576,1024]{1,0:T(8,128)S(1)} %get-tuple-element.53.state, f32[512,1024]{1,0:T(8,128)S(1)} %get-tuple-element.57.partial, f32[512,1024]{1,0:T(8,128)S(1)} %get-tuple-element.58.product, bf16[96,1024]{1,0:T(8,128)(2,1)S(1)} %copy-done.3), custom_call_target="tpu_custom_call" | custom-call | flops 1073741824 | tf_op jit(solution)/shard_map/advance3/pallas_call | solution.py:350
Async XLA Ops:
  0.1 6.4 %copy-start.1 = (bf16[1024,128]{1,0:T(8,128)(2,1)S(1)}, bf16[1024,128]{1,0:T(8,128)(2,1)}, u32[]{:S(2)}) copy-start(bf16[1024,128]{1,0:T(8,128)(2,1)} %constant.19.clone.left) | copy-start | bytes 786436
  2.1 18.6 %collective-permute-start.3 = (f32[96,1024]{1,0:T(8,128)S(1)}, f32[96,1024]{1,0:T(8,128)S(1)}, u32[]{:S(2)}, u32[]{:S(2)}) collective-permute-start(f32[96,1024]{1,0:T(8,128)S(1)} %get-tuple-element.36.to_pair), channel_id=1, source_target_pairs={{0,2},{2,0},{4,6},{6,4},{8,10},{10,8},{12,14},{14,12},{16,18},{18,... | collective-permute-start | bytes 1179656 | tf_op jit(solution)/shard_map/ppermute | solution.py:385
  2.2 18.5 %collective-permute-start.4 = (f32[96,1024]{1,0:T(8,128)S(1)}, f32[96,1024]{1,0:T(8,128)S(1)}, u32[]{:S(2)}, u32[]{:S(2)}) collective-permute-start(f32[96,1024]{1,0:T(8,128)S(1)} %get-tuple-element.37.to_other), channel_id=1, source_target_pairs={{0,254},{2,4},{4,2},{6,8},{8,6},{10,12},{12,10},{14,16},{16,14},{1... | collective-permute-start | bytes 1179656 | tf_op jit(solution)/shard_map/ppermute | solution.py:386
  7.5 14.8 %collective-permute-start.1 = (f32[24,64]{1,0:T(8,128)S(1)}, f32[24,64]{1,0:T(8,128)S(1)}, u32[]{:S(2)}, u32[]{:S(2)}) collective-permute-start(f32[24,64]{1,0:T(8,128)S(1)} %get-tuple-element.38), channel_id=1, source_target_pairs={{0,126},{2,132},{4,130},{6,136},{8,134},{10,140},{12,138},{14,144}... | collective-permute-start | bytes 18440 | tf_op jit(solution)/shard_map/ppermute | solution.py:391
  10.2 12.1 %collective-permute-start.2 = (f32[24,64]{1,0:T(8,128)S(1)}, f32[24,64]{1,0:T(8,128)S(1)}, u32[]{:S(2)}, u32[]{:S(2)}) collective-permute-start(f32[24,64]{1,0:T(8,128)S(1)} %get-tuple-element.39), channel_id=1, source_target_pairs={{0,130},{2,128},{4,134},{6,132},{8,138},{10,136},{12,142},{14,140}... | collective-permute-start | bytes 18440 | tf_op jit(solution)/shard_map/ppermute | solution.py:392
  11.3 8.5 %copy-start.4 = (f32[1024]{0:T(1024)S(1)}, f32[1024]{0:T(1024)}, u32[]{:S(2)}) copy-start(f32[1024]{0:T(1024)} %param.6) | copy-start | bytes 12292
  16.5 4.1 %copy-start = (bf16[1152,1024]{1,0:T(8,128)(2,1)S(1)}, bf16[1152,1024]{1,0:T(8,128)(2,1)}, u32[]{:S(2)}) copy-start(bf16[1152,1024]{1,0:T(8,128)(2,1)} %constant.18.clone.near) | copy-start | bytes 7077892
  16.5 4.1 %copy-start.2 = (bf16[1024,128]{1,0:T(8,128)(2,1)S(1)}, bf16[1024,128]{1,0:T(8,128)(2,1)}, u32[]{:S(2)}) copy-start(bf16[1024,128]{1,0:T(8,128)(2,1)} %constant.19.clone.left) | copy-start | bytes 786436
  16.5 5.7 %collective-permute-start = (f32[24,512]{1,0:T(8,128)S(1)}, f32[24,512]{1,0:T(8,128)S(1)}, u32[]{:S(2)}, u32[]{:S(2)}) collective-permute-start(f32[24,512]{1,0:T(8,128)S(1)} %get-tuple-element.35), channel_id=1, source_target_pairs={{0,128},{2,130},{4,132},{6,134},{8,136},{10,138},{12,140},{14,142}... | collective-permute-start | bytes 147464 | tf_op jit(solution)/shard_map/ppermute | solution.py:397
  20.6 1.7 %copy-start.3 = (bf16[96,1024]{1,0:T(8,128)(2,1)S(1)}, bf16[96,1024]{1,0:T(8,128)(2,1)}, u32[]{:S(2)}) copy-start(bf16[96,1024]{1,0:T(8,128)(2,1)} %constant.20.clone.right) | copy-start | bytes 589828
  24.4 6.3 %collective-permute-start.5 = (f32[24,576]{1,0:T(8,128)S(1)}, f32[24,576]{1,0:T(8,128)S(1)}, u32[]{:S(2)}, u32[]{:S(2)}) collective-permute-start(f32[24,576]{1,0:T(8,128)S(1)} %get-tuple-element.45), channel_id=1, source_target_pairs={{0,128},{2,130},{4,132},{6,134},{8,136},{10,138},{12,140},{14,142}... | collective-permute-start | bytes 165896 | tf_op jit(solution)/shard_map/ppermute | solution.py:414
  32.1 5.7 %collective-permute-start.6 = (f32[24,512]{1,0:T(8,128)S(1)}, f32[24,512]{1,0:T(8,128)S(1)}, u32[]{:S(2)}, u32[]{:S(2)}) collective-permute-start(f32[24,512]{1,0:T(8,128)S(1)} %get-tuple-element.52), channel_id=1, source_target_pairs={{0,128},{2,130},{4,132},{6,134},{8,136},{10,138},{12,140},{14,142}... | collective-permute-start | bytes 147464 | tf_op jit(solution)/shard_map/ppermute | solution.py:423

commit v2 on v1

--- a/solution.py
+++ b/solution.py
@@ -131,67 +131,9 @@
     return window[32 : 32 + count, :] - courant[:, cols] * total
 
 
-def fetch(pairs, sems):
-    copies = [pltpu.make_async_copy(source, target, sems.at[i]) for i, (source, target) in enumerate(pairs)]
-    for copy in copies:
-        copy.start()
-    return copies
-
-
-def await_all(copies):
-    for copy in copies:
-        copy.wait()
-
-
-def own_section(wedge, near, left, state, product, proj):
-    for at in range(0, 64, 16):
-        rows = jnp.swapaxes(wedge[:, at : at + 16, :], 0, 1).reshape(16 * lines, -1)
-        state[at * lines : (at + 16) * lines, :] = rows
-    hi, lo = halves(state[...])
-    parts = projected(hi, lo, left)
-    proj[...] = far_values(parts)
-    for t in range(4):
-        product[:, columns_of(t)] = near_tile(t, hi, lo, parts, near)
-
-
-def ends_kernel(place, to_pair, to_other, left, proj_pair, proj_other, rows):
-    @pl.when(place[0] == 0)
-    def _():
-        rows[:64, :] = to_pair[32:, :]
-        rows[64:, :] = to_other[:64, :]
-
-    @pl.when(place[0] != 0)
-    def _():
-        rows[:64, :] = to_pair[:64, :]
-        rows[64:, :] = to_other[32:, :]
-
-    hi, lo = halves(rows[...])
-    values = far_values(projected(hi, lo, left))
-    proj_pair[...] = values[:, :64]
-    proj_other[...] = values[:, 64:]
-
-
-def inside_kernel(state, courant, partial):
-    for lane in range(8):
-        for at in range(0, 448, 112):
-            partial[at : at + 112, columns_of(lane, 128)] = azimuth(state, courant, at, 14, lane)
-
-
-def launch_kernel(place, field, near, left, to_pair, to_other, *refs):
-    outs, (wedge, *here, sems) = refs[:3], refs[3:]
-    first, middle, last = slice(0, 16), slice(16, 48), slice(48, 64)
-    edges = fetch([(field.at[:, span, :], wedge.at[:, span, :]) for span in (first, last)], sems)
-
-    def others():
-        return [(field.at[:, middle, :], wedge.at[:, middle, :])] + list(zip((near, left), here))
-
-    @pl.when(place[1] != 0)
-    def _():
-        fetch(others(), sems.at[2:])
-
-    await_all(edges)
-    low = jnp.swapaxes(wedge[:, first, :], 0, 1)[:halo].reshape(halo * lines, -1)
-    high = jnp.swapaxes(wedge[:, last, :], 0, 1)[16 - halo :].reshape(halo * lines, -1)
+def launch_kernel(place, field, to_pair, to_other):
+    low = jnp.swapaxes(field[:, :16, :], 0, 1)[:halo].reshape(halo * lines, -1)
+    high = jnp.swapaxes(field[:, 48:, :], 0, 1)[16 - halo :].reshape(halo * lines, -1)
 
     @pl.when(place[0] == 0)
     def _():
@@ -203,24 +145,35 @@
         to_pair[...] = low
         to_other[...] = high
 
-    @pl.when(place[1] != 0)
-    def _():
-        await_all([pltpu.make_async_copy(*ends, sems.at[2 + i]) for i, ends in enumerate(others())])
-        own_section(wedge, *here, *outs)
-
-
-def own_kernel(place, field, near, left, *refs):
-    done, outs, (wedge, *here, sems) = refs[:3], refs[3:6], refs[6:]
-
-    @pl.when(place[1] == 0)
-    def _():
-        await_all(fetch([(field, wedge)] + list(zip((near, left), here)), sems))
-        own_section(wedge, *here, *outs)
-
-    @pl.when(place[1] != 0)
-    def _():
-        for out, ready in zip(outs, done):
-            out[...] = ready[...]
+
+def own_kernel(place, field, left, state, hi_out, lo_out, parts_out, proj, proj_pair, proj_other):
+    done = []
+    for t in range(4):
+        cols = columns_of(t)
+        rows = jnp.swapaxes(field[:, :, cols], 0, 1).reshape(state.shape[0], tile)
+        done.append(write_state(t, rows, left, state, hi_out, lo_out, parts_out, 0))
+    values = far_values(done)
+    proj[...] = values
+    low, high = values[:, :64], values[:, -64:]
+
+    @pl.when(place[0] == 0)
+    def _():
+        proj_pair[...] = high
+        proj_other[...] = low
+
+    @pl.when(place[0] != 0)
+    def _():
+        proj_pair[...] = low
+        proj_other[...] = high
+
+
+def inside_kernel(state, hi, lo, parts, courant, near, partial, product):
+    pieces = [parts[:, columns_of(t, 128)] for t in range(4)]
+    for t in range(4):
+        product[:, columns_of(t)] = near_tile(t, hi, lo, pieces, near)
+        for lane in (2 * t, 2 * t + 1):
+            for at in range(0, 448, 112):
+                partial[at : at + 112, columns_of(lane, 128)] = azimuth(state, courant, at, 14, lane)
 
 
 def join_kernel(place, from_pair, from_other, own, courant, near, left, sides, partial, product):
@@ -276,82 +229,87 @@
     return jnp.concatenate([hi, lo, hi, lo], axis=0).astype(bf16).T
 
 
-def advanced_rows(partial, state, product, stack_rows, right):
-    return partial + state * (product + dot(stack_rows, right[...]))
-
-
-def finish(ahead, left, hi_out, lo_out, parts_out, proj):
-    inner = proj.shape[1]
-    hi, lo = halves(ahead[32 : 32 + inner, :])
-    hi_out[...] = hi
-    lo_out[...] = lo
-    parts = projected(hi, lo, left)
-    for t in range(4):
-        parts_out[:, columns_of(t, 128)] = parts[t]
-    proj[...] = far_values(parts)
+def write_state(t, rows, left, ahead, hi_out, lo_out, parts_out, skip=32):
+    cols = columns_of(t)
+    ahead[:, cols] = rows
+    inner = parts_out.shape[0]
+    hi, lo = halves(rows[skip : skip + inner])
+    hi_out[:, cols] = hi
+    lo_out[:, cols] = lo
+    part = dot(hi, left[cols, :]) + dot(lo, left[cols, :])
+    parts_out[:, columns_of(t, 128)] = part
+    return part
 
 
 def first_kernel(place, opposite, by_other, by_pair, own, partial, product, sides, side_partial, side_product,
-                 right, left, ahead, hi, lo, parts, proj, ends):
+                 right, left, ahead, hi, lo, parts, proj, stack):
+    stack[64:576, :] = opposite_stack(opposite[...], 1.0)
     near_pair = opposite_stack(by_pair[...], 1.0)
     near_other = opposite_stack(by_other[...], 1.0)
 
     @pl.when(place[0] == 0)
     def _():
-        ends[0] = near_other
-        ends[1] = near_pair
+        stack[:64, :] = near_other
+        stack[576:, :] = near_pair
 
     @pl.when(place[0] != 0)
     def _():
-        ends[0] = near_pair
-        ends[1] = near_other
-
-    stack = opposite_stack(opposite[...], 1.0)
-    ahead[:64, :] = advanced_rows(side_partial[0, :64], sides[0, 32:96], side_product[0], ends[0], right)
-    ahead[576:, :] = advanced_rows(side_partial[1, 32:], sides[1, 64:128], side_product[1], ends[1], right)
-    low = side_partial[0, 64:]
-    high = side_partial[1, :32]
-    for at in range(0, 512, 128):
-        inside = partial[max(at - 32, 0) : min(at + 96, 448)]
-        if at == 0:
-            inside = jnp.concatenate([low, inside], axis=0)
-        if at == 384:
-            inside = jnp.concatenate([inside, high], axis=0)
-        rows = slice(at, at + 128)
-        ahead[64 + at : 192 + at, :] = advanced_rows(inside, own[rows], product[rows], stack[rows], right)
-    finish(ahead, left, hi, lo, parts, proj)
+        stack[:64, :] = near_pair
+        stack[576:, :] = near_other
+
+    done = []
+    for t in range(4):
+        cols = columns_of(t)
+        far = dot(stack[...], right[:, cols])
+        low = side_partial[0, :64, cols] + sides[0, 32:96, cols] * (side_product[0, :, cols] + far[:64])
+        high = side_partial[1, 32:, cols] + sides[1, 64:128, cols] * (side_product[1, :, cols] + far[576:])
+        inside = jnp.concatenate(
+            [side_partial[0, 64:, cols], partial[:, cols], side_partial[1, :32, cols]], axis=0
+        )
+        middle = inside + own[:, cols] * (product[:, cols] + far[64:576])
+        rows = jnp.concatenate([low, middle, high], axis=0)
+        done.append(write_state(t, rows, left, ahead, hi, lo, parts))
+    proj[...] = far_values(done)
 
 
 def second_kernel(new, opposite, state, partial, product, right, left, ahead, hi, lo, parts, proj):
     stack = opposite_stack(opposite[...], new)
-    step = 144
-    for at in range(0, ahead.shape[0], step):
-        rows = slice(at, at + step)
-        ahead[rows, :] = advanced_rows(
-            partial[rows], state[32 + at : 32 + at + step], product[rows], stack[rows], right
-        )
-    finish(ahead, left, hi, lo, parts, proj)
-
-
-def last_kernel(new, opposite, state, partial, product, right, out):
+    count = ahead.shape[0]
+    done = []
+    for t in range(4):
+        cols = columns_of(t)
+        far = dot(stack, right[:, cols])
+        rows = partial[:, cols] + state[32 : 32 + count, cols] * (product[:, cols] + far)
+        done.append(write_state(t, rows, left, ahead, hi, lo, parts))
+    proj[...] = far_values(done)
+
+
+def last_kernel(new, opposite, state, partial, product, right, out, done, sems):
     stack = opposite_stack(opposite[...], new)
-    for at in range(0, 512, 64):
-        rows = slice(at, at + 64)
-        done = advanced_rows(partial[rows], state[32 + at : 96 + at], product[rows], stack[rows], right)
-        out[:, at // 8 : at // 8 + 8, :] = jnp.swapaxes(done.reshape(8, lines, -1), 0, 1)
+    count = partial.shape[0]
+    copies = []
+    for t in range(4):
+        cols = columns_of(t)
+        far = dot(stack, right[:, cols])
+        rows = partial[:, cols] + state[32 : 32 + count, cols] * (product[:, cols] + far)
+        done[:, :, cols] = jnp.swapaxes(rows.reshape(count // lines, lines, tile), 0, 1)
+        copies.append(pltpu.make_async_copy(done.at[:, :, cols], out.at[:, :, cols], sems.at[t]))
+        copies[-1].start()
+    for copy in copies:
+        copy.wait()
 
 
 def shape_of(*dims, dtype=f32):
     return jax.ShapeDtypeStruct(dims, dtype)
 
 
-def run(kernel, outs, *args, name, flops, scalars=0, away=(), scratch=()):
+def run(kernel, outs, *args, name, flops, scalars=0, away=(), out_away=False, scratch=()):
     spaces = [pltpu.SMEM if i < scalars else pltpu.HBM if i in away else pltpu.VMEM for i in range(len(args))]
     return pl.pallas_call(
         kernel,
         out_shape=outs,
         in_specs=[pl.BlockSpec(memory_space=space) for space in spaces],
-        out_specs=jax.tree.map(lambda _: pl.BlockSpec(memory_space=pltpu.VMEM), outs),
+        out_specs=jax.tree.map(lambda _: pl.BlockSpec(memory_space=pltpu.HBM if out_away else pltpu.VMEM), outs),
         scratch_shapes=scratch,
         compiler_params=pltpu.CompilerParams(vmem_limit_bytes=16 << 20),
         cost_estimate=pl.CostEstimate(flops=flops, transcendentals=0, bytes_accessed=0),
@@ -371,45 +329,37 @@
     far_other = [(i, (i + half + (1 if i % 2 else -1)) % size) for i in range(size)]
     near, left, right = (jnp.asarray(t) for t in tables(count))
     index = lax.axis_index("theta").astype(jnp.int32)
-    place = jnp.stack([index & 1, jnp.where((index & 14) == 14, 0, 1)])
+    place = (index & 1).reshape(1)
     speed = courant.reshape(1, count)
     edge = shape_of(halo * lines, count)
 
-    own_shapes = [shape_of(cells, count), shape_of(cells, count), shape_of(rank, cells)]
-    at_rest = [pltpu.with_memory_space_constraint(a, pltpu.HBM) for a in (field, near, left)]
-    room = [pltpu.VMEM(a.shape, a.dtype) for a in at_rest]
-    to_pair, to_other, *early = run(
-        launch_kernel, [edge, edge] + own_shapes, place, *at_rest, scalars=1, away=(1, 2, 3), name="launch",
-        flops=1 << 30, scratch=room + [pltpu.SemaphoreType.DMA((5,))],
-    )
+    def state_shapes(rows, inner):
+        return [shape_of(rows, count), shape_of(inner, count, dtype=bf16), shape_of(inner, count, dtype=bf16),
+                shape_of(inner, 512), shape_of(rank, inner)]
+
+    to_pair, to_other = run(launch_kernel, [edge, edge], place, field, scalars=1, name="launch", flops=0)
     from_pair = lax.ppermute(to_pair, "theta", pair)
     from_other = lax.ppermute(to_other, "theta", other)
-    proj_pair, proj_other = run(
-        ends_kernel, [shape_of(rank, 64)] * 2, place, to_pair, to_other, left,
-        scalars=1, name="ends", flops=0, scratch=[pltpu.VMEM((128, count), f32)],
+    own, hi, lo, parts, proj, proj_pair, proj_other = run(
+        own_kernel, state_shapes(cells, cells) + [shape_of(rank, 64)] * 2, place, field, left,
+        scalars=1, name="own", flops=1 << 30,
     )
     by_other = lax.ppermute(proj_other, "theta", far_other)
     by_pair = lax.ppermute(proj_pair, "theta", far_pair)
-    own, product, proj = run(
-        own_kernel, own_shapes, place, *at_rest, *early, scalars=1, away=(1, 2, 3), name="own",
-        flops=4 << 30, scratch=room + [pltpu.SemaphoreType.DMA((3,))],
-    )
     proj = lax.ppermute(proj, "theta", opposite)
-    partial = run(inside_kernel, shape_of(cells - 64, count), own, speed, name="inside", flops=0)
+    partial, product = run(
+        inside_kernel, [shape_of(cells - 64, count), shape_of(cells, count)],
+        own, hi, lo, parts, speed, near, name="inside", flops=4 << 30,
+    )
     sides, side_partial, side_product = run(
         join_kernel, [shape_of(2, 160, count), shape_of(2, 96, count), shape_of(2, 64, count)],
         place, from_pair, from_other, own, speed, near, left, scalars=1, name="join", flops=1 << 30,
     )
 
-    def advanced_shapes(rows):
-        inner = rows - 64
-        return [shape_of(rows, count), shape_of(inner, count, dtype=bf16), shape_of(inner, count, dtype=bf16),
-                shape_of(inner, 512), shape_of(rank, inner)]
-
     first, hi, lo, parts, proj = run(
-        first_kernel, advanced_shapes(cells + 128),
+        first_kernel, state_shapes(cells + 128, cells + 64),
         place, proj, by_other, by_pair, own, partial, product, sides, side_partial, side_product, right, left,
-        scalars=1, scratch=[pltpu.VMEM((2, 64, 4 * rank), bf16)], name="advance1", flops=1 << 30,
+        scalars=1, scratch=[pltpu.VMEM((cells + 128, 4 * rank), bf16)], name="advance1", flops=1 << 30,
     )
     proj = lax.ppermute(proj, "theta", opposite)
     partial, product = run(
@@ -417,7 +367,7 @@
         first, hi, lo, parts, own, sides, speed, near, name="rate2", flops=3 << 30,
     )
     second, hi, lo, parts, proj = run(
-        functools.partial(second_kernel, 0.25), advanced_shapes(cells + 64),
+        functools.partial(second_kernel, 0.25), state_shapes(cells + 64, cells),
         proj, first, partial, product, right, left, name="advance2", flops=1 << 30,
     )
     proj = lax.ppermute(proj, "theta", opposite)
@@ -427,7 +377,8 @@
     )
     return run(
         functools.partial(last_kernel, 2.0 / 3.0), shape_of(*field.shape),
-        proj, second, partial, product, right, name="advance3", flops=1 << 30,
+        proj, second, partial, product, right, name="advance3", flops=1 << 30, out_away=True,
+        scratch=[pltpu.VMEM(field.shape, f32), pltpu.SemaphoreType.DMA((4,))],
     )
 
 

time: 40.2 us -> 36.6 us (0.910)
  the two profiles are of different devices: /device:TPU:230 before, /device:TPU:8 now
where the time goes in v2:
time: 36.6 us; the launch traced here: 36.2 us
  Pallas kernels  15.1 us (41%)
  starting transfers between devices  14.4 us (39%)
  waiting for transfers between devices  4.8 us (13%)
  local copies, waits for them, and re-layouts  1.66 us (5%)
    pallas_call x9, Pallas kernels, run(): pl.pallas_call(kernel, out_shape=outs, in_specs=[pl.BlockSpec(memory_spac...  15.1 us
    ppermute x1, starting transfers between devices, body(): from_other = lax.ppermute(to_other, 'theta', other)  9.88 us
    ppermute x3, starting transfers between devices, body(): proj = lax.ppermute(proj, 'theta', opposite)  4.27 us
    ppermute x3, waiting for transfers between devices, body(): proj = lax.ppermute(proj, 'theta', opposite)  3.09 us
    unnamed x10, local copies, waits for them, and re-layouts  1.66 us
    ppermute x1, waiting for transfers between devices, body(): by_other = lax.ppermute(proj_other, 'theta', far_other)  1.06 us
  transfers between devices with their start and end apart: 7, of which 4 were waited for; matrix products, arithmetic and copies ran while one was open for 0% of the time, Pallas kernels for 28%

profile of v2, /device:TPU:8, one launch (start us, length us, event | category | flops | bytes accessed | tf_op | source)
XLA Modules:
  0.0 36.2 jit_solution(13153465449756681910)
XLA Ops:
  0.0 0.0 copy-start.1
  0.0 0.0 copy-start.2
  0.0 1.6 %copy-done.2 = f32[8,64,1024]{2,1,0:T(8,128)S(1)} copy-done((f32[8,64,1024]{2,1,0:T(8,128)S(1)}, f32[8,64,1024]{2,1,0:T(8,128)}, u32[]{:S(2)}) %copy-start.2) | copy-done | bytes 2097176
  1.6 0.2 launch.1
  1.8 0.0 copy-start
  1.8 0.0 copy-start.4
  1.9 0.1 collective-permute-start.3
  2.0 9.9 %collective-permute-start.4 = (f32[96,1024]{1,0:T(8,128)S(1)}, f32[96,1024]{1,0:T(8,128)S(1)}, u32[]{:S(2)}, u32[]{:S(2)}) collective-permute-start(f32[96,1024]{1,0:T(8,128)S(1)} %get-tuple-element.43), channel_id=1, source_target_pairs={{0,254},{2,4},{4,2},{6,8},{8,6},{10,12},{12,10},{14,16},{16,14},{1... | collective-permute-start | bytes 1179656 | tf_op jit(solution)/shard_map/ppermute | solution.py:342
  11.8 0.0 copy-done.1
  11.8 1.2 %own.1 = (f32[512,1024]{1,0:T(8,128)S(1)}, bf16[512,1024]{1,0:T(8,128)(2,1)S(1)}, bf16[512,1024]{1,0:T(8,128)(2,1)S(1)}, f32[512,512]{1,0:T(8,128)S(1)}, f32[24,...) custom-call(s32[1]{0:T(128)} %bitcast.place, f32[8,64,1024]{2,1,0:T(8,128)S(1)} %copy-done.2, ...), custom_call_target="tpu_custom_call" | custom-call | flops 1073741824 | tf_op jit(solution)/shard_map/own/pallas_call | solution.py:308
  13.0 0.1 collective-permute-start.1
  13.1 0.1 collective-permute-start.2
  13.2 1.3 %collective-permute-start = (f32[24,512]{1,0:T(8,128)S(1)}, f32[24,512]{1,0:T(8,128)S(1)}, u32[]{:S(2)}, u32[]{:S(2)}) collective-permute-start(f32[24,512]{1,0:T(8,128)S(1)} %get-tuple-element.33), channel_id=1, source_target_pairs={{0,128},{2,130},{4,132},{6,134},{8,136},{10,138},{12,140},{14,142}... | collective-permute-start | bytes 147464 | tf_op jit(solution)/shard_map/ppermute | solution.py:349
  14.5 0.0 copy-done
  14.5 0.0 copy-done.4
  14.5 2.2 %inside.1 = (f32[448,1024]{1,0:T(8,128)S(1)}, f32[512,1024]{1,0:T(8,128)S(1)}) custom-call(f32[512,1024]{1,0:T(8,128)S(1)} %get-tuple-element.36.state.own, bf16[512,1024]{1,0:T(8,128)(2,1)S(1)} %get-tuple-element.37.hi, bf16[512,1024]{1,0:T(8,128)(2,1)S(1)} %get-tuple-element.38.lo, f32[512,512]{1,0:T(8,128)S(1)} %get-tuple-element.39.parts, ...), custom_call_target="tpu_custom_call" | custom-call | flops 4294967296 | tf_op jit(solution)/shard_map/inside/pallas_call | solution.py:308
  16.7 0.0 copy-start.3
  16.7 0.0 collective-permute-done.3.from_pair
  16.8 0.6 %collective-permute-done.4.from_other = f32[96,1024]{1,0:T(8,128)S(1)} collective-permute-done((f32[96,1024]{1,0:T(8,128)S(1)}, f32[96,1024]{1,0:T(8,128)S(1)}, u32[]{:S(2)}, u32[]{:S(2)}) %collective-permute-start.4) | collective-permute-done | bytes 393248 | tf_op jit(solution)/shard_map/ppermute | solution.py:342
  17.4 1.0 %join.1 = (f32[2,160,1024]{2,1,0:T(8,128)S(1)}, f32[2,96,1024]{2,1,0:T(8,128)S(1)}, f32[2,64,1024]{2,1,0:T(8,128)S(1)}) custom-call(s32[1]{0:T(128)} %bitcast.place, f32[96,1024]{1,0:T(8,128)S(1)} %collective-permute-done.3.from_pair, f32[96,1024]{1,0:T(8,128)S(1)} %collective-permute-done.4.from_other, f32[512,1024]{1,0:T(8,128)S(1)} %get-tuple-element.36.state.own, ...), custom_call_target="tpu_custom_call" | custom-call | flops 1073741824 | tf_op jit(solution)/shard_map/join/pallas_call | solution.py:308
  18.4 1.1 %collective-permute-done.1.by_other = f32[24,64]{1,0:T(8,128)S(1)} collective-permute-done((f32[24,64]{1,0:T(8,128)S(1)}, f32[24,64]{1,0:T(8,128)S(1)}, u32[]{:S(2)}, u32[]{:S(2)}) %collective-permute-start.1) | collective-permute-done | bytes 6176 | tf_op jit(solution)/shard_map/ppermute | solution.py:347
  19.5 0.0 collective-permute-done.2.by_pair
  19.5 0.0 collective-permute-done.opposite
  19.5 0.0 copy-done.3
  19.5 1.6 %advance1.1 = (f32[640,1024]{1,0:T(8,128)S(1)}, bf16[576,1024]{1,0:T(8,128)(2,1)S(1)}, bf16[576,1024]{1,0:T(8,128)(2,1)S(1)}, f32[576,512]{1,0:T(8,128)S(1)}, f32[24,576]{1,0:T(8,128)S(1)}) custom-call(s32[1]{0:T(128)} %bitcast.place, f32[24,512]{1,0:T(8,128)S(1)} %collective-permute-done.opposite, f32[24,64]{1,0:T(8,128)S(1)} %collective-permute-done.1.by_other, ...), custom_call_target="tpu_custom_call" | custom-call | flops 1073741824 | tf_op jit(solution)/shard_map/advance1/pallas_call | solution.py:308
  21.1 1.5 %collective-permute-start.5 = (f32[24,576]{1,0:T(8,128)S(1)}, f32[24,576]{1,0:T(8,128)S(1)}, u32[]{:S(2)}, u32[]{:S(2)}) collective-permute-start(f32[24,576]{1,0:T(8,128)S(1)} %get-tuple-element.47), channel_id=1, source_target_pairs={{0,128},{2,130},{4,132},{6,134},{8,136},{10,138},{12,140},{14,142}... | collective-permute-start | bytes 165896 | tf_op jit(solution)/shard_map/ppermute | solution.py:364
  22.6 2.9 %rate2.1 = (f32[576,1024]{1,0:T(8,128)S(1)}, f32[576,1024]{1,0:T(8,128)S(1)}) custom-call(f32[640,1024]{1,0:T(8,128)S(1)} %get-tuple-element.48.state, bf16[576,1024]{1,0:T(8,128)(2,1)S(1)} %get-tuple-element.49.hi, bf16[576,1024]{1,0:T(8,128)(2,1)S(1)} %get-tuple-element.50.lo, f32[576,512]{1,0:T(8,128)S(1)} %get-tuple-element.51.parts, ...), custom_call_target="tpu_custom_call" | custom-call | flops 3221225472 | tf_op jit(solution)/shard_map/rate2/pallas_call | solution.py:308
  25.5 1.7 %collective-permute-done.5.opposite = f32[24,576]{1,0:T(8,128)S(1)} collective-permute-done((f32[24,576]{1,0:T(8,128)S(1)}, f32[24,576]{1,0:T(8,128)S(1)}, u32[]{:S(2)}, u32[]{:S(2)}) %collective-permute-start.5) | collective-permute-done | bytes 55328 | tf_op jit(solution)/shard_map/ppermute | solution.py:364
  27.2 1.3 %advance2.1 = (f32[576,1024]{1,0:T(8,128)S(1)}, bf16[512,1024]{1,0:T(8,128)(2,1)S(1)}, bf16[512,1024]{1,0:T(8,128)(2,1)S(1)}, f32[512,512]{1,0:T(8,128)S(1)}, f32[24,512]{1,0:T(8,128)S(1)}) custom-call(f32[24,576]{1,0:T(8,128)S(1)} %collective-permute-done.5.opposite, f32[640,1024]{1,0:T(8,128)S(1)} %get-tuple-element.48.state, ...), custom_call_target="tpu_custom_call" | custom-call | flops 1073741824 | tf_op jit(solution)/shard_map/advance2/pallas_call | solution.py:308
  28.4 1.4 %collective-permute-start.6 = (f32[24,512]{1,0:T(8,128)S(1)}, f32[24,512]{1,0:T(8,128)S(1)}, u32[]{:S(2)}, u32[]{:S(2)}) collective-permute-start(f32[24,512]{1,0:T(8,128)S(1)} %get-tuple-element.54), channel_id=1, source_target_pairs={{0,128},{2,130},{4,132},{6,134},{8,136},{10,138},{12,140},{14,142}... | collective-permute-start | bytes 147464 | tf_op jit(solution)/shard_map/ppermute | solution.py:373
  29.9 2.8 %rate3.1 = (f32[512,1024]{1,0:T(8,128)S(1)}, f32[512,1024]{1,0:T(8,128)S(1)}) custom-call(f32[576,1024]{1,0:T(8,128)S(1)} %get-tuple-element.55.state, bf16[512,1024]{1,0:T(8,128)(2,1)S(1)} %get-tuple-element.56.hi, bf16[512,1024]{1,0:T(8,128)(2,1)S(1)} %get-tuple-element.57.lo, f32[512,512]{1,0:T(8,128)S(1)} %get-tuple-element.58.parts, ...), custom_call_target="tpu_custom_call" | custom-call | flops 3221225472 | tf_op jit(solution)/shard_map/rate3/pallas_call | solution.py:308
  32.7 1.4 %collective-permute-done.6.opposite = f32[24,512]{1,0:T(8,128)S(1)} collective-permute-done((f32[24,512]{1,0:T(8,128)S(1)}, f32[24,512]{1,0:T(8,128)S(1)}, u32[]{:S(2)}, u32[]{:S(2)}) %collective-permute-start.6) | collective-permute-done | bytes 49184 | tf_op jit(solution)/shard_map/ppermute | solution.py:373
  34.1 1.9 %advance3.1 = f32[8,64,1024]{2,1,0:T(8,128)} custom-call(f32[24,512]{1,0:T(8,128)S(1)} %collective-permute-done.6.opposite, f32[576,1024]{1,0:T(8,128)S(1)} %get-tuple-element.55.state, f32[512,1024]{1,0:T(8,128)S(1)} %get-tuple-element.59.partial, f32[512,1024]{1,0:T(8,128)S(1)} %get-tuple-element.60.product, bf16[96,1024]{1,0:T(8,128)(2,1)S(1)} %copy-done.3), custom_call_target="tpu_custom_call" | custom-call | flops 1073741824 | tf_op jit(solution)/shard_map/advance3/pallas_call | solution.py:308
Async XLA Ops:
  0.0 11.8 %copy-start.1 = (bf16[1024,128]{1,0:T(8,128)(2,1)S(1)}, bf16[1024,128]{1,0:T(8,128)(2,1)}, u32[]{:S(2)}) copy-start(bf16[1024,128]{1,0:T(8,128)(2,1)} %constant.15.clone.left) | copy-start | bytes 786436
  0.0 1.6 %copy-start.2 = (f32[8,64,1024]{2,1,0:T(8,128)S(1)}, f32[8,64,1024]{2,1,0:T(8,128)}, u32[]{:S(2)}) copy-start(f32[8,64,1024]{2,1,0:T(8,128)} %field.3) | copy-start | bytes 6291460
  1.8 12.7 %copy-start = (bf16[1152,1024]{1,0:T(8,128)(2,1)S(1)}, bf16[1152,1024]{1,0:T(8,128)(2,1)}, u32[]{:S(2)}) copy-start(bf16[1152,1024]{1,0:T(8,128)(2,1)} %constant.14.clone.near) | copy-start | bytes 7077892
  1.8 12.7 %copy-start.4 = (f32[1024]{0:T(1024)S(1)}, f32[1024]{0:T(1024)}, u32[]{:S(2)}) copy-start(f32[1024]{0:T(1024)} %param.6) | copy-start | bytes 12292
  1.9 14.9 %collective-permute-start.3 = (f32[96,1024]{1,0:T(8,128)S(1)}, f32[96,1024]{1,0:T(8,128)S(1)}, u32[]{:S(2)}, u32[]{:S(2)}) collective-permute-start(f32[96,1024]{1,0:T(8,128)S(1)} %get-tuple-element.42), channel_id=1, source_target_pairs={{0,2},{2,0},{4,6},{6,4},{8,10},{10,8},{12,14},{14,12},{16,18},{18,... | collective-permute-start | bytes 1179656 | tf_op jit(solution)/shard_map/ppermute | solution.py:341
  2.0 15.4 %collective-permute-start.4 = (f32[96,1024]{1,0:T(8,128)S(1)}, f32[96,1024]{1,0:T(8,128)S(1)}, u32[]{:S(2)}, u32[]{:S(2)}) collective-permute-start(f32[96,1024]{1,0:T(8,128)S(1)} %get-tuple-element.43), channel_id=1, source_target_pairs={{0,254},{2,4},{4,2},{6,8},{8,6},{10,12},{12,10},{14,16},{16,14},{1... | collective-permute-start | bytes 1179656 | tf_op jit(solution)/shard_map/ppermute | solution.py:342
  13.0 6.5 %collective-permute-start.1 = (f32[24,64]{1,0:T(8,128)S(1)}, f32[24,64]{1,0:T(8,128)S(1)}, u32[]{:S(2)}, u32[]{:S(2)}) collective-permute-start(f32[24,64]{1,0:T(8,128)S(1)} %get-tuple-element.34), channel_id=1, source_target_pairs={{0,126},{2,132},{4,130},{6,136},{8,134},{10,140},{12,138},{14,144}... | collective-permute-start | bytes 18440 | tf_op jit(solution)/shard_map/ppermute | solution.py:347
  13.1 6.4 %collective-permute-start.2 = (f32[24,64]{1,0:T(8,128)S(1)}, f32[24,64]{1,0:T(8,128)S(1)}, u32[]{:S(2)}, u32[]{:S(2)}) collective-permute-start(f32[24,64]{1,0:T(8,128)S(1)} %get-tuple-element.35), channel_id=1, source_target_pairs={{0,130},{2,128},{4,134},{6,132},{8,138},{10,136},{12,142},{14,140}... | collective-permute-start | bytes 18440 | tf_op jit(solution)/shard_map/ppermute | solution.py:348
  13.2 6.3 %collective-permute-start = (f32[24,512]{1,0:T(8,128)S(1)}, f32[24,512]{1,0:T(8,128)S(1)}, u32[]{:S(2)}, u32[]{:S(2)}) collective-permute-start(f32[24,512]{1,0:T(8,128)S(1)} %get-tuple-element.33), channel_id=1, source_target_pairs={{0,128},{2,130},{4,132},{6,134},{8,136},{10,138},{12,140},{14,142}... | collective-permute-start | bytes 147464 | tf_op jit(solution)/shard_map/ppermute | solution.py:349
  16.7 2.8 %copy-start.3 = (bf16[96,1024]{1,0:T(8,128)(2,1)S(1)}, bf16[96,1024]{1,0:T(8,128)(2,1)}, u32[]{:S(2)}) copy-start(bf16[96,1024]{1,0:T(8,128)(2,1)} %constant.16.clone.right) | copy-start | bytes 589828
  21.1 6.1 %collective-permute-start.5 = (f32[24,576]{1,0:T(8,128)S(1)}, f32[24,576]{1,0:T(8,128)S(1)}, u32[]{:S(2)}, u32[]{:S(2)}) collective-permute-start(f32[24,576]{1,0:T(8,128)S(1)} %get-tuple-element.47), channel_id=1, source_target_pairs={{0,128},{2,130},{4,132},{6,134},{8,136},{10,138},{12,140},{14,142}... | collective-permute-start | bytes 165896 | tf_op jit(solution)/shard_map/ppermute | solution.py:364
  28.4 5.7 %collective-permute-start.6 = (f32[24,512]{1,0:T(8,128)S(1)}, f32[24,512]{1,0:T(8,128)S(1)}, u32[]{:S(2)}, u32[]{:S(2)}) collective-permute-start(f32[24,512]{1,0:T(8,128)S(1)} %get-tuple-element.54), channel_id=1, source_target_pairs={{0,128},{2,130},{4,132},{6,134},{8,136},{10,138},{12,140},{14,142}... | collective-permute-start | bytes 147464 | tf_op jit(solution)/shard_map/ppermute | solution.py:373

commit v3 on v2

--- a/solution.py
+++ b/solution.py
@@ -108,14 +108,14 @@
     return both[:rank] + both[64 : 64 + rank]
 
 
-def near_tile(t, hi, lo, parts, near):
+def near_tile(t, rows, parts, near):
     place = lax.broadcasted_iota(jnp.int32, parts[0].shape, 1) % 64
     halves_sum = parts[2] + parts[3] if t < 2 else parts[0] + parts[1]
     values = jnp.where(place < rank + block_rank, halves_sum, parts[t ^ 1])
     value_hi, value_lo = halves(values)
-    cols = columns_of(t)
-    left = jnp.concatenate([hi[:, cols], lo[:, cols], hi[:, cols], value_hi, value_lo, value_hi], axis=1)
-    return dot(left, near[:, cols])
+    hi, lo = halves(rows)
+    left = jnp.concatenate([hi, lo, hi, value_hi, value_lo, value_hi], axis=1)
+    return dot(left, near[:, columns_of(t)])
 
 
 def azimuth(state, courant, start, cells, lane):
@@ -131,62 +131,76 @@
     return window[32 : 32 + count, :] - courant[:, cols] * total
 
 
-def launch_kernel(place, field, to_pair, to_other):
-    low = jnp.swapaxes(field[:, :16, :], 0, 1)[:halo].reshape(halo * lines, -1)
-    high = jnp.swapaxes(field[:, 48:, :], 0, 1)[16 - halo :].reshape(halo * lines, -1)
-
-    @pl.when(place[0] == 0)
+def even():
+    return lax.rem(lax.axis_index("theta"), 2) == 0
+
+
+def launch_kernel(field, to_pair, to_other, wedge, sems):
+    spans = (slice(0, 16), slice(48, 64), slice(16, 48))
+    copies = [
+        pltpu.make_async_copy(field.at[:, span, :], wedge.at[:, span, :], sems.at[i]) for i, span in enumerate(spans)
+    ]
+    for copy in copies:
+        copy.start()
+    for copy in copies[:2]:
+        copy.wait()
+    low = jnp.swapaxes(wedge[:, :16, :], 0, 1)[:halo].reshape(halo * lines, -1)
+    high = jnp.swapaxes(wedge[:, 48:, :], 0, 1)[16 - halo :].reshape(halo * lines, -1)
+
+    @pl.when(even())
     def _():
         to_pair[...] = high
         to_other[...] = low
 
-    @pl.when(place[0] != 0)
+    @pl.when(jnp.logical_not(even()))
     def _():
         to_pair[...] = low
         to_other[...] = high
 
-
-def own_kernel(place, field, left, state, hi_out, lo_out, parts_out, proj, proj_pair, proj_other):
+    copies[2].wait()
+
+
+def own_kernel(field, left, state, parts_out, proj, proj_pair, proj_other):
     done = []
     for t in range(4):
         cols = columns_of(t)
         rows = jnp.swapaxes(field[:, :, cols], 0, 1).reshape(state.shape[0], tile)
-        done.append(write_state(t, rows, left, state, hi_out, lo_out, parts_out, 0))
+        done.append(write_state(t, rows, left, state, parts_out, 0))
     values = far_values(done)
     proj[...] = values
     low, high = values[:, :64], values[:, -64:]
 
-    @pl.when(place[0] == 0)
+    @pl.when(even())
     def _():
         proj_pair[...] = high
         proj_other[...] = low
 
-    @pl.when(place[0] != 0)
+    @pl.when(jnp.logical_not(even()))
     def _():
         proj_pair[...] = low
         proj_other[...] = high
 
 
-def inside_kernel(state, hi, lo, parts, courant, near, partial, product):
+def inside_kernel(state, parts, courant, near, partial, product):
     pieces = [parts[:, columns_of(t, 128)] for t in range(4)]
     for t in range(4):
-        product[:, columns_of(t)] = near_tile(t, hi, lo, pieces, near)
+        product[:, columns_of(t)] = near_tile(t, state[:, columns_of(t)], pieces, near)
         for lane in (2 * t, 2 * t + 1):
             for at in range(0, 448, 112):
                 partial[at : at + 112, columns_of(lane, 128)] = azimuth(state, courant, at, 14, lane)
 
 
-def join_kernel(place, from_pair, from_other, own, courant, near, left, sides, partial, product):
+def join_kernel(from_pair, from_other, own, courant, near, left, sides, partial, product):
     wide = halo * lines
     sides[0, wide:, :] = own[:64, :]
     sides[1, :64, :] = own[448:, :]
 
-    @pl.when(place[0] == 0)
+    @pl.when(even())
     def _():
         sides[0, :wide, :] = from_other[...]
         sides[1, 64:, :] = from_pair[...]
 
-    @pl.when(place[0] != 0)
+    @pl.when(jnp.logical_not(even()))
     def _():
         sides[0, :wide, :] = from_pair[...]
         sides[1, 64:, :] = from_other[...]
@@ -195,7 +209,7 @@
     hi, lo = halves(rows)
     parts = projected(hi, lo, left)
     for t in range(4):
-        both = near_tile(t, hi, lo, parts, near)
+        both = near_tile(t, rows[:, columns_of(t)], parts, near)
         product[0, :, columns_of(t)] = both[:64]
         product[1, :, columns_of(t)] = both[64:]
     for lane in range(8):
@@ -203,12 +217,12 @@
             partial[side, :, columns_of(lane, 128)] = azimuth(sides.at[side], courant, 0, 12, lane)
 
 
-def rate_kernel(old, new, cells, state, hi, lo, parts, own, sides, courant, near, partial, product):
+def rate_kernel(old, new, cells, state, parts, own, sides, courant, near, partial, product):
     count = partial.shape[0]
     extra = (count - own.shape[0]) // 2
     pieces = [parts[:, columns_of(t, 128)] for t in range(4)]
     for t in range(4):
-        product[:, columns_of(t)] = new * near_tile(t, hi, lo, pieces, near)
+        product[:, columns_of(t)] = new * near_tile(t, state[32 : 32 + count, columns_of(t)], pieces, near)
         for lane in (2 * t, 2 * t + 1):
             cols = columns_of(lane, 128)
             for at in range(0, count, cells * lines):
@@ -229,30 +243,28 @@
     return jnp.concatenate([hi, lo, hi, lo], axis=0).astype(bf16).T
 
 
-def write_state(t, rows, left, ahead, hi_out, lo_out, parts_out, skip=32):
+def write_state(t, rows, left, ahead, parts_out, skip=32):
     cols = columns_of(t)
     ahead[:, cols] = rows
     inner = parts_out.shape[0]
     hi, lo = halves(rows[skip : skip + inner])
-    hi_out[:, cols] = hi
-    lo_out[:, cols] = lo
     part = dot(hi, left[cols, :]) + dot(lo, left[cols, :])
     parts_out[:, columns_of(t, 128)] = part
     return part
 
 
-def first_kernel(place, opposite, by_other, by_pair, own, partial, product, sides, side_partial, side_product,
-                 right, left, ahead, hi, lo, parts, proj, stack):
+def first_kernel(opposite, by_other, by_pair, own, partial, product, sides, side_partial, side_product,
+                 right, left, ahead, parts, proj, stack):
     stack[64:576, :] = opposite_stack(opposite[...], 1.0)
     near_pair = opposite_stack(by_pair[...], 1.0)
     near_other = opposite_stack(by_other[...], 1.0)
 
-    @pl.when(place[0] == 0)
+    @pl.when(even())
     def _():
         stack[:64, :] = near_other
         stack[576:, :] = near_pair
 
-    @pl.when(place[0] != 0)
+    @pl.when(jnp.logical_not(even()))
     def _():
         stack[:64, :] = near_pair
         stack[576:, :] = near_other
@@ -268,11 +280,11 @@
         )
         middle = inside + own[:, cols] * (product[:, cols] + far[64:576])
         rows = jnp.concatenate([low, middle, high], axis=0)
-        done.append(write_state(t, rows, left, ahead, hi, lo, parts))
+        done.append(write_state(t, rows, left, ahead, parts))
     proj[...] = far_values(done)
 
 
-def second_kernel(new, opposite, state, partial, product, right, left, ahead, hi, lo, parts, proj):
+def second_kernel(new, opposite, state, partial, product, right, left, ahead, parts, proj):
     stack = opposite_stack(opposite[...], new)
     count = ahead.shape[0]
     done = []
@@ -280,7 +292,7 @@
         cols = columns_of(t)
         far = dot(stack, right[:, cols])
         rows = partial[:, cols] + state[32 : 32 + count, cols] * (product[:, cols] + far)
-        done.append(write_state(t, rows, left, ahead, hi, lo, parts))
+        done.append(write_state(t, rows, left, ahead, parts))
     proj[...] = far_values(done)
 
 
@@ -288,12 +300,12 @@
     stack = opposite_stack(opposite[...], new)
     count = partial.shape[0]
     copies = []
-    for t in range(4):
-        cols = columns_of(t)
+    for start, width in ((0, 256), (256, 256), (512, 256), (768, 128), (896, 128)):
+        cols = slice(start, start + width)
         far = dot(stack, right[:, cols])
         rows = partial[:, cols] + state[32 : 32 + count, cols] * (product[:, cols] + far)
-        done[:, :, cols] = jnp.swapaxes(rows.reshape(count // lines, lines, tile), 0, 1)
-        copies.append(pltpu.make_async_copy(done.at[:, :, cols], out.at[:, :, cols], sems.at[t]))
+        done[:, :, cols] = jnp.swapaxes(rows.reshape(count // lines, lines, width), 0, 1)
+        copies.append(pltpu.make_async_copy(done.at[:, :, cols], out.at[:, :, cols], sems.at[len(copies)]))
         copies[-1].start()
     for copy in copies:
         copy.wait()
@@ -303,8 +315,8 @@
     return jax.ShapeDtypeStruct(dims, dtype)
 
 
-def run(kernel, outs, *args, name, flops, scalars=0, away=(), out_away=False, scratch=()):
-    spaces = [pltpu.SMEM if i < scalars else pltpu.HBM if i in away else pltpu.VMEM for i in range(len(args))]
+def run(kernel, outs, *args, name, flops, away=(), out_away=False, scratch=()):
+    spaces = [pltpu.HBM if i in away else pltpu.VMEM for i in range(len(args))]
     return pl.pallas_call(
         kernel,
         out_shape=outs,
@@ -328,57 +340,57 @@
     far_pair = [(i, (i + half + (-1 if i % 2 else 1)) % size) for i in range(size)]
     far_other = [(i, (i + half + (1 if i % 2 else -1)) % size) for i in range(size)]
     near, left, right = (jnp.asarray(t) for t in tables(count))
-    index = lax.axis_index("theta").astype(jnp.int32)
-    place = (index & 1).reshape(1)
     speed = courant.reshape(1, count)
     edge = shape_of(halo * lines, count)
 
     def state_shapes(rows, inner):
-        return [shape_of(rows, count), shape_of(inner, count, dtype=bf16), shape_of(inner, count, dtype=bf16),
-                shape_of(inner, 512), shape_of(rank, inner)]
-
-    to_pair, to_other = run(launch_kernel, [edge, edge], place, field, scalars=1, name="launch", flops=0)
+        return [shape_of(rows, count), shape_of(inner, 512), shape_of(rank, inner)]
+
+    to_pair, to_other, wedge = run(
+        launch_kernel, [edge, edge, shape_of(*field.shape)], pltpu.with_memory_space_constraint(field, pltpu.HBM),
+        away=(0,), name="launch", flops=0, scratch=[pltpu.SemaphoreType.DMA((3,))],
+    )
     from_pair = lax.ppermute(to_pair, "theta", pair)
     from_other = lax.ppermute(to_other, "theta", other)
-    own, hi, lo, parts, proj, proj_pair, proj_other = run(
-        own_kernel, state_shapes(cells, cells) + [shape_of(rank, 64)] * 2, place, field, left,
-        scalars=1, name="own", flops=1 << 30,
+    own, parts, proj, proj_pair, proj_other = run(
+        own_kernel, state_shapes(cells, cells) + [shape_of(rank, 64)] * 2, wedge, left,
+        name="own", flops=1 << 30,
     )
     by_other = lax.ppermute(proj_other, "theta", far_other)
     by_pair = lax.ppermute(proj_pair, "theta", far_pair)
     proj = lax.ppermute(proj, "theta", opposite)
     partial, product = run(
         inside_kernel, [shape_of(cells - 64, count), shape_of(cells, count)],
-        own, hi, lo, parts, speed, near, name="inside", flops=4 << 30,
+        own, parts, speed, near, name="inside", flops=4 << 30,
     )
     sides, side_partial, side_product = run(
         join_kernel, [shape_of(2, 160, count), shape_of(2, 96, count), shape_of(2, 64, count)],
-        place, from_pair, from_other, own, speed, near, left, scalars=1, name="join", flops=1 << 30,
-    )
-
-    first, hi, lo, parts, proj = run(
+        from_pair, from_other, own, speed, near, left, name="join", flops=1 << 30,
+    )
+
+    first, parts, proj = run(
         first_kernel, state_shapes(cells + 128, cells + 64),
-        place, proj, by_other, by_pair, own, partial, product, sides, side_partial, side_product, right, left,
-        scalars=1, scratch=[pltpu.VMEM((cells + 128, 4 * rank), bf16)], name="advance1", flops=1 << 30,
+        proj, by_other, by_pair, own, partial, product, sides, side_partial, side_product, right, left,
+        scratch=[pltpu.VMEM((cells + 128, 4 * rank), bf16)], name="advance1", flops=1 << 30,
     )
     proj = lax.ppermute(proj, "theta", opposite)
     partial, product = run(
         functools.partial(rate_kernel, 0.75, 0.25, 12), [shape_of(cells + 64, count)] * 2,
-        first, hi, lo, parts, own, sides, speed, near, name="rate2", flops=3 << 30,
-    )
-    second, hi, lo, parts, proj = run(
+        first, parts, own, sides, speed, near, name="rate2", flops=3 << 30,
+    )
+    second, parts, proj = run(
         functools.partial(second_kernel, 0.25), state_shapes(cells + 64, cells),
         proj, first, partial, product, right, left, name="advance2", flops=1 << 30,
     )
     proj = lax.ppermute(proj, "theta", opposite)
     partial, product = run(
         functools.partial(rate_kernel, 1.0 / 3.0, 2.0 / 3.0, 16), [shape_of(cells, count)] * 2,
-        second, hi, lo, parts, own, sides, speed, near, name="rate3", flops=3 << 30,
+        second, parts, own, sides, speed, near, name="rate3", flops=3 << 30,
     )
     return run(
         functools.partial(last_kernel, 2.0 / 3.0), shape_of(*field.shape),
         proj, second, partial, product, right, name="advance3", flops=1 << 30, out_away=True,
-        scratch=[pltpu.VMEM(field.shape, f32), pltpu.SemaphoreType.DMA((4,))],
+        scratch=[pltpu.VMEM(field.shape, f32), pltpu.SemaphoreType.DMA((5,))],
     )
 
 

time: 36.6 us -> 36.3 us (level)
  local copies, waits for them, and re-layouts: 1.66 us -> 0.02 us
  Pallas kernels: 15.1 us -> 16.4 us
    unnamed x10 -> x8, local copies, waits for them, and re-layouts: 1.66 us -> 0.02 us
    pallas_call x9, Pallas kernels: 15.1 us -> 16.4 us  [run(): pl.pallas_call(kernel, out_shape=outs, in_specs=[pl.BlockSpec(memory_spac...]
where the time goes in v3:
time: 36.3 us; the launch traced here: 35.8 us
  Pallas kernels  16.4 us (45%)
  starting transfers between devices  14.4 us (40%)
  waiting for transfers between devices  4.77 us (13%)
    pallas_call x9, Pallas kernels, run(): pl.pallas_call(kernel, out_shape=outs, in_specs=[pl.BlockSpec(memory_spac...  16.4 us
    ppermute x1, starting transfers between devices, body(): from_other = lax.ppermute(to_other, 'theta', other)  9.88 us
    ppermute x3, starting transfers between devices, body(): proj = lax.ppermute(proj, 'theta', opposite)  4.23 us
    ppermute x3, waiting for transfers between devices, body(): proj = lax.ppermute(proj, 'theta', opposite)  3.11 us
    ppermute x1, waiting for transfers between devices, body(): by_other = lax.ppermute(proj_other, 'theta', far_other)  0.95 us
  transfers between devices with their start and end apart: 7, of which 4 were waited for; matrix products, arithmetic and copies ran while one was open for 0% of the time, Pallas kernels for 28%

profile of v3, /device:TPU:8, one launch (start us, length us, event | category | flops | bytes accessed | tf_op | source)
XLA Modules:
  0.0 35.8 jit_solution(18004511380840448840)
XLA Ops:
  0.0 0.0 copy-start.1
  0.0 1.6 %launch.1 = (f32[96,1024]{1,0:T(8,128)S(1)}, f32[96,1024]{1,0:T(8,128)S(1)}, f32[8,64,1024]{2,1,0:T(8,128)S(1)}) custom-call(f32[8,64,1024]{2,1,0:T(8,128)} %field.1), custom_call_target="tpu_custom_call" | custom-call | tf_op jit(solution)/shard_map/launch/pallas_call | solution.py:320
  1.6 0.0 copy-start
  1.6 0.0 copy-start.3
  1.6 0.1 collective-permute-start.3
  1.7 9.9 %collective-permute-start.4 = (f32[96,1024]{1,0:T(8,128)S(1)}, f32[96,1024]{1,0:T(8,128)S(1)}, u32[]{:S(2)}, u32[]{:S(2)}) collective-permute-start(f32[96,1024]{1,0:T(8,128)S(1)} %get-tuple-element.37), channel_id=1, source_target_pairs={{0,254},{2,4},{4,2},{6,8},{8,6},{10,12},{12,10},{14,16},{16,14},{1... | collective-permute-start | bytes 1179656 | tf_op jit(solution)/shard_map/ppermute | solution.py:354
  11.6 0.0 copy-done.1
  11.6 1.1 %own.1 = (f32[512,1024]{1,0:T(8,128)S(1)}, f32[512,512]{1,0:T(8,128)S(1)}, f32[24,512]{1,0:T(8,128)S(1)}, f32[24,64]{1,0:T(8,128)S(1)}, f32[24,64]{1,0:T(8,128)S(1)}) custom-call(f32[8,64,1024]{2,1,0:T(8,128)S(1)} %get-tuple-element.28.field, bf16[1024,128]{1,0:T(8,128)(2,1)S(1)} %copy-done.1), custom_call_target="tpu_custom_call" | custom-call | flops 1073741824 | tf_op jit(solution)/shard_map/own/pallas_call | solution.py:320
  12.7 0.1 collective-permute-start.1
  12.8 0.1 collective-permute-start.2
  12.9 1.3 %collective-permute-start = (f32[24,512]{1,0:T(8,128)S(1)}, f32[24,512]{1,0:T(8,128)S(1)}, u32[]{:S(2)}, u32[]{:S(2)}) collective-permute-start(f32[24,512]{1,0:T(8,128)S(1)} %get-tuple-element.29), channel_id=1, source_target_pairs={{0,128},{2,130},{4,132},{6,134},{8,136},{10,138},{12,140},{14,142}... | collective-permute-start | bytes 147464 | tf_op jit(solution)/shard_map/ppermute | solution.py:361
  14.2 0.0 copy-done
  14.2 0.0 copy-done.3
  14.2 2.2 %inside.1 = (f32[448,1024]{1,0:T(8,128)S(1)}, f32[512,1024]{1,0:T(8,128)S(1)}) custom-call(f32[512,1024]{1,0:T(8,128)S(1)} %get-tuple-element.32.state.own, f32[512,512]{1,0:T(8,128)S(1)} %get-tuple-element.33.parts, f32[1,1024]{1,0:T(1,128)S(1)} %bitcast.1, bf16[1152,1024]{1,0:T(8,128)(2,1)S(1)} %copy-done), custom_call_target="tpu_custom_call" | custom-call | flops 4294967296 | tf_op jit(solution)/shard_map/inside/pallas_call | solution.py:320
  16.5 0.0 copy-start.2
  16.5 0.0 collective-permute-done.3.from_pair
  16.5 0.7 %collective-permute-done.4.from_other = f32[96,1024]{1,0:T(8,128)S(1)} collective-permute-done((f32[96,1024]{1,0:T(8,128)S(1)}, f32[96,1024]{1,0:T(8,128)S(1)}, u32[]{:S(2)}, u32[]{:S(2)}) %collective-permute-start.4) | collective-permute-done | bytes 393248 | tf_op jit(solution)/shard_map/ppermute | solution.py:354
  17.2 1.1 %join.1 = (f32[2,160,1024]{2,1,0:T(8,128)S(1)}, f32[2,96,1024]{2,1,0:T(8,128)S(1)}, f32[2,64,1024]{2,1,0:T(8,128)S(1)}) custom-call(f32[96,1024]{1,0:T(8,128)S(1)} %collective-permute-done.3.from_pair, f32[96,1024]{1,0:T(8,128)S(1)} %collective-permute-done.4.from_other, f32[512,1024]{1,0:T(8,128)S(1)} %get-tuple-element.32.state.own, ...), custom_call_target="tpu_custom_call" | custom-call | flops 1073741824 | tf_op jit(solution)/shard_map/join/pallas_call | solution.py:320
  18.3 0.9 %collective-permute-done.1.by_other = f32[24,64]{1,0:T(8,128)S(1)} collective-permute-done((f32[24,64]{1,0:T(8,128)S(1)}, f32[24,64]{1,0:T(8,128)S(1)}, u32[]{:S(2)}, u32[]{:S(2)}) %collective-permute-start.1) | collective-permute-done | bytes 6176 | tf_op jit(solution)/shard_map/ppermute | solution.py:359
  19.2 0.0 collective-permute-done.2.by_pair
  19.2 0.0 collective-permute-done.opposite
  19.2 0.0 copy-done.2
  19.2 1.5 %advance1.1 = (f32[640,1024]{1,0:T(8,128)S(1)}, f32[576,512]{1,0:T(8,128)S(1)}, f32[24,576]{1,0:T(8,128)S(1)}) custom-call(f32[24,512]{1,0:T(8,128)S(1)} %collective-permute-done.opposite, f32[24,64]{1,0:T(8,128)S(1)} %collective-permute-done.1.by_other, f32[24,64]{1,0:T(8,128)S(1)} %collective-permute-done.2.by_pair, ...), custom_call_target="tpu_custom_call" | custom-call | flops 1073741824 | tf_op jit(solution)/shard_map/advance1/pallas_call | solution.py:320
  20.7 1.5 %collective-permute-start.5 = (f32[24,576]{1,0:T(8,128)S(1)}, f32[24,576]{1,0:T(8,128)S(1)}, u32[]{:S(2)}, u32[]{:S(2)}) collective-permute-start(f32[24,576]{1,0:T(8,128)S(1)} %get-tuple-element.41), channel_id=1, source_target_pairs={{0,128},{2,130},{4,132},{6,134},{8,136},{10,138},{12,140},{14,142}... | collective-permute-start | bytes 165896 | tf_op jit(solution)/shard_map/ppermute | solution.py:376
  22.3 3.0 %rate2.1 = (f32[576,1024]{1,0:T(8,128)S(1)}, f32[576,1024]{1,0:T(8,128)S(1)}) custom-call(f32[640,1024]{1,0:T(8,128)S(1)} %get-tuple-element.42.state, f32[576,512]{1,0:T(8,128)S(1)} %get-tuple-element.43.parts, f32[512,1024]{1,0:T(8,128)S(1)} %get-tuple-element.32.state.own, f32[2,160,1024]{2,1,0:T(8,128)S(1)} %get-tuple-element.38.sides, ...), custom_call_target="tpu_custom_call" | custom-call | flops 3221225472 | tf_op jit(solution)/shard_map/rate2/pallas_call | solution.py:320
  25.2 1.6 %collective-permute-done.5.opposite = f32[24,576]{1,0:T(8,128)S(1)} collective-permute-done((f32[24,576]{1,0:T(8,128)S(1)}, f32[24,576]{1,0:T(8,128)S(1)}, u32[]{:S(2)}, u32[]{:S(2)}) %collective-permute-start.5) | collective-permute-done | bytes 55328 | tf_op jit(solution)/shard_map/ppermute | solution.py:376
  26.9 1.2 %advance2.1 = (f32[576,1024]{1,0:T(8,128)S(1)}, f32[512,512]{1,0:T(8,128)S(1)}, f32[24,512]{1,0:T(8,128)S(1)}) custom-call(f32[24,576]{1,0:T(8,128)S(1)} %collective-permute-done.5.opposite, f32[640,1024]{1,0:T(8,128)S(1)} %get-tuple-element.42.state, f32[576,1024]{1,0:T(8,128)S(1)} %get-tuple-element.44.partial, f32[576,1024]{1,0:T(8,128)S(1)} %get-tuple-element.45.product, ...), custom_call_target="tpu_custom_call" | custom-call | flops 1073741824 | tf_op jit(solution)/shard_map/advance2/pallas_call | solution.py:320
  28.1 1.4 %collective-permute-start.6 = (f32[24,512]{1,0:T(8,128)S(1)}, f32[24,512]{1,0:T(8,128)S(1)}, u32[]{:S(2)}, u32[]{:S(2)}) collective-permute-start(f32[24,512]{1,0:T(8,128)S(1)} %get-tuple-element.46), channel_id=1, source_target_pairs={{0,128},{2,130},{4,132},{6,134},{8,136},{10,138},{12,140},{14,142}... | collective-permute-start | bytes 147464 | tf_op jit(solution)/shard_map/ppermute | solution.py:385
  29.5 2.8 %rate3.1 = (f32[512,1024]{1,0:T(8,128)S(1)}, f32[512,1024]{1,0:T(8,128)S(1)}) custom-call(f32[576,1024]{1,0:T(8,128)S(1)} %get-tuple-element.47.state, f32[512,512]{1,0:T(8,128)S(1)} %get-tuple-element.48.parts, f32[512,1024]{1,0:T(8,128)S(1)} %get-tuple-element.32.state.own, f32[2,160,1024]{2,1,0:T(8,128)S(1)} %get-tuple-element.38.sides, ...), custom_call_target="tpu_custom_call" | custom-call | flops 3221225472 | tf_op jit(solution)/shard_map/rate3/pallas_call | solution.py:320
  32.3 1.5 %collective-permute-done.6.opposite = f32[24,512]{1,0:T(8,128)S(1)} collective-permute-done((f32[24,512]{1,0:T(8,128)S(1)}, f32[24,512]{1,0:T(8,128)S(1)}, u32[]{:S(2)}, u32[]{:S(2)}) %collective-permute-start.6) | collective-permute-done | bytes 49184 | tf_op jit(solution)/shard_map/ppermute | solution.py:385
  33.8 1.9 %advance3.1 = f32[8,64,1024]{2,1,0:T(8,128)} custom-call(f32[24,512]{1,0:T(8,128)S(1)} %collective-permute-done.6.opposite, f32[576,1024]{1,0:T(8,128)S(1)} %get-tuple-element.47.state, f32[512,1024]{1,0:T(8,128)S(1)} %get-tuple-element.49.partial, f32[512,1024]{1,0:T(8,128)S(1)} %get-tuple-element.50.product, bf16[96,1024]{1,0:T(8,128)(2,1)S(1)} %copy-done.2), custom_call_target="tpu_custom_call" | custom-call | flops 1073741824 | tf_op jit(solution)/shard_map/advance3/pallas_call | solution.py:320
Async XLA Ops:
  0.0 11.6 %copy-start.1 = (bf16[1024,128]{1,0:T(8,128)(2,1)S(1)}, bf16[1024,128]{1,0:T(8,128)(2,1)}, u32[]{:S(2)}) copy-start(bf16[1024,128]{1,0:T(8,128)(2,1)} %constant.7.clone.left) | copy-start | bytes 786436
  1.6 12.6 %copy-start = (bf16[1152,1024]{1,0:T(8,128)(2,1)S(1)}, bf16[1152,1024]{1,0:T(8,128)(2,1)}, u32[]{:S(2)}) copy-start(bf16[1152,1024]{1,0:T(8,128)(2,1)} %constant.6.clone.near) | copy-start | bytes 7077892
  1.6 12.6 %copy-start.3 = (f32[1024]{0:T(1024)S(1)}, f32[1024]{0:T(1024)}, u32[]{:S(2)}) copy-start(f32[1024]{0:T(1024)} %param.6) | copy-start | bytes 12292
  1.6 14.8 %collective-permute-start.3 = (f32[96,1024]{1,0:T(8,128)S(1)}, f32[96,1024]{1,0:T(8,128)S(1)}, u32[]{:S(2)}, u32[]{:S(2)}) collective-permute-start(f32[96,1024]{1,0:T(8,128)S(1)} %get-tuple-element.36), channel_id=1, source_target_pairs={{0,2},{2,0},{4,6},{6,4},{8,10},{10,8},{12,14},{14,12},{16,18},{18,... | collective-permute-start | bytes 1179656 | tf_op jit(solution)/shard_map/ppermute | solution.py:353
  1.7 15.4 %collective-permute-start.4 = (f32[96,1024]{1,0:T(8,128)S(1)}, f32[96,1024]{1,0:T(8,128)S(1)}, u32[]{:S(2)}, u32[]{:S(2)}) collective-permute-start(f32[96,1024]{1,0:T(8,128)S(1)} %get-tuple-element.37), channel_id=1, source_target_pairs={{0,254},{2,4},{4,2},{6,8},{8,6},{10,12},{12,10},{14,16},{16,14},{1... | collective-permute-start | bytes 1179656 | tf_op jit(solution)/shard_map/ppermute | solution.py:354
  12.7 6.5 %collective-permute-start.1 = (f32[24,64]{1,0:T(8,128)S(1)}, f32[24,64]{1,0:T(8,128)S(1)}, u32[]{:S(2)}, u32[]{:S(2)}) collective-permute-start(f32[24,64]{1,0:T(8,128)S(1)} %get-tuple-element.30), channel_id=1, source_target_pairs={{0,126},{2,132},{4,130},{6,136},{8,134},{10,140},{12,138},{14,144}... | collective-permute-start | bytes 18440 | tf_op jit(solution)/shard_map/ppermute | solution.py:359
  12.8 6.4 %collective-permute-start.2 = (f32[24,64]{1,0:T(8,128)S(1)}, f32[24,64]{1,0:T(8,128)S(1)}, u32[]{:S(2)}, u32[]{:S(2)}) collective-permute-start(f32[24,64]{1,0:T(8,128)S(1)} %get-tuple-element.31), channel_id=1, source_target_pairs={{0,130},{2,128},{4,134},{6,132},{8,138},{10,136},{12,142},{14,140}... | collective-permute-start | bytes 18440 | tf_op jit(solution)/shard_map/ppermute | solution.py:360
  12.9 6.3 %collective-permute-start = (f32[24,512]{1,0:T(8,128)S(1)}, f32[24,512]{1,0:T(8,128)S(1)}, u32[]{:S(2)}, u32[]{:S(2)}) collective-permute-start(f32[24,512]{1,0:T(8,128)S(1)} %get-tuple-element.29), channel_id=1, source_target_pairs={{0,128},{2,130},{4,132},{6,134},{8,136},{10,138},{12,140},{14,142}... | collective-permute-start | bytes 147464 | tf_op jit(solution)/shard_map/ppermute | solution.py:361
  16.5 2.8 %copy-start.2 = (bf16[96,1024]{1,0:T(8,128)(2,1)S(1)}, bf16[96,1024]{1,0:T(8,128)(2,1)}, u32[]{:S(2)}) copy-start(bf16[96,1024]{1,0:T(8,128)(2,1)} %constant.8.clone.right) | copy-start | bytes 589828
  20.7 6.1 %collective-permute-start.5 = (f32[24,576]{1,0:T(8,128)S(1)}, f32[24,576]{1,0:T(8,128)S(1)}, u32[]{:S(2)}, u32[]{:S(2)}) collective-permute-start(f32[24,576]{1,0:T(8,128)S(1)} %get-tuple-element.41), channel_id=1, source_target_pairs={{0,128},{2,130},{4,132},{6,134},{8,136},{10,138},{12,140},{14,142}... | collective-permute-start | bytes 165896 | tf_op jit(solution)/shard_map/ppermute | solution.py:376
  28.1 5.7 %collective-permute-start.6 = (f32[24,512]{1,0:T(8,128)S(1)}, f32[24,512]{1,0:T(8,128)S(1)}, u32[]{:S(2)}, u32[]{:S(2)}) collective-permute-start(f32[24,512]{1,0:T(8,128)S(1)} %get-tuple-element.46), channel_id=1, source_target_pairs={{0,128},{2,130},{4,132},{6,134},{8,136},{10,138},{12,140},{14,142}... | collective-permute-start | bytes 147464 | tf_op jit(solution)/shard_map/ppermute | solution.py:385
